TPU v7x, 1024 devices: a whole 4x4x32 slice. The times are simulated.
1024 devices in a mesh: ctx: 64 (over z_lo, y, core), tp: 4 (over z_hi), rep: 4 (over x).
Axes of the slice: x: 4, y: 4, z: 32 (z_hi: 4, z_lo: 8; z = z_hi * 8 + z_lo), core: 2. Of those that a mesh axis runs over, the one named last changes fastest.
Arguments:
- queries: bfloat16 [49152, 4096], P(('ctx', 'rep'), 'tp'), may hold values from -6 to 6
- key_states: bfloat16 [49152, 1024], P(('ctx', 'rep'), 'tp'), may hold values from -6 to 6
- value_states: bfloat16 [49152, 1024], P(('ctx', 'rep'), 'tp'), may hold values from -6 to 6
- out_grad: bfloat16 [49152, 4096], P(('ctx', 'rep'), 'tp'), may hold values from -6 to 6
- doc_lengths: int32 [255], replicated, may hold values from 0 to 768, as said below
Outputs:
- attended: bfloat16 [49152, 4096], P(('ctx', 'rep'), 'tp')
- query_grad: bfloat16 [49152, 4096], P(('ctx', 'rep'), 'tp')
- key_grad: bfloat16 [49152, 1024], P(('ctx', 'rep'), 'tp')
- value_grad: bfloat16 [49152, 1024], P(('ctx', 'rep'), 'tp')
Inputs may be any that keep to these rules, and one draw needn't show every extreme that they name: `doc_lengths`: the lengths sum to 49152; the largest is exactly 768; some entries are 0.
All inputs are finite; a program needn't handle non-finite values.
Results may differ from a plain program's by a relative error of at most 0.007.
Values may be sent and summed in bfloat16 or wider, within the bound.
No kernel may reach another device: no remote copies, remote signals or barrier semaphores. Data moves between devices by JAX's collectives and lax.ppermute only.
A program may use at most 64 MiB of HBM per device.

v0:
```python
import math

import jax
import jax.numpy as jnp
from jax import lax
from jax.sharding import PartitionSpec as P

HD = 128
REACH = 4


masked_score = -1e30


def from_behind(block, axis, distance):
    devices = range(lax.axis_size(axis))
    route = [(i - distance, i) for i in devices if i - distance in devices]
    return lax.ppermute(block, axis, route)


def document_of(doc_ends, positions):
    return jnp.sum((doc_ends[None, :] <= positions[:, None]).astype(jnp.int32), axis=1)


def per_device(queries, key_states, value_states, out_grad, doc_lengths):
    seq_rows = queries.shape[0]
    key_width = key_states.shape[1]
    kv_heads = key_width // HD
    group_size = queries.shape[1] // HD // kv_heads
    scaling = 1.0 / math.sqrt(HD)
    position = lax.axis_index(("ctx", "rep"))
    doc_ends = jnp.cumsum(doc_lengths)
    own_pair = (key_states, value_states)
    received = []
    for distance in range(1, REACH + 1):
        received.append(from_behind((own_pair[0], own_pair[1]), ("ctx", "rep"), distance))
    first_pos = position * seq_rows
    local_pos = first_pos + jnp.arange(seq_rows, dtype=jnp.int32)
    query_doc = document_of(doc_ends, local_pos)

    def allowed_for(key_pos):
        same_doc = document_of(doc_ends, key_pos)[None, :] == query_doc[:, None]
        return same_doc & (key_pos[None, :] <= local_pos[:, None]) & (key_pos[None, :] >= 0)

    block_total = REACH + 1
    key_blocks = [received[REACH - 1 - index][0] for index in range(REACH)] + [key_states]
    value_blocks = [received[REACH - 1 - index][1] for index in range(REACH)] + [value_states]
    block_masks = [
        allowed_for(local_pos - (REACH - index) * seq_rows) for index in range(block_total)
    ]
    attended_cols = []
    query_cols = []
    key_parts = [[] for index in range(block_total)]
    value_parts = [[] for index in range(block_total)]
    for group in range(kv_heads):
        low_col = group * group_size * HD
        high_col = (group + 1) * group_size * HD
        query_group = queries[:, low_col:high_col].reshape(seq_rows, group_size, HD)
        grad_group = out_grad[:, low_col:high_col].reshape(seq_rows, group_size, HD)
        group_keys = [blk[:, group * HD : (group + 1) * HD] for blk in key_blocks]
        group_values = [blk[:, group * HD : (group + 1) * HD] for blk in value_blocks]
        score_blocks = []
        for block_id in range(block_total):

            def score_fn(key_block=group_keys[block_id], block_mask=block_masks[block_id]):
                raw_scores = (
                    jnp.einsum(
                        "tjd,sd->jts", query_group, key_block, preferred_element_type=jnp.float32
                    )
                    * scaling
                )
                return jnp.where(block_mask[None], raw_scores, masked_score)

            score_blocks.append(score_fn())
        row_max = jnp.max(score_blocks[0], axis=-1, keepdims=True)
        for block_id in range(1, block_total):
            row_max = jnp.maximum(row_max, jnp.max(score_blocks[block_id], axis=-1, keepdims=True))
        exp_total = sum(
            (
                jnp.sum(jnp.exp(block_score - row_max), axis=-1, keepdims=True)
                for block_score in score_blocks
            )
        )
        log_total = row_max + jnp.log(exp_total)
        prob_blocks = [jnp.exp(block_score - log_total) for block_score in score_blocks]
        prob_bf_blocks = [block_prob.astype(jnp.bfloat16) for block_prob in prob_blocks]
        attended_acc = jnp.zeros((seq_rows, group_size, HD), jnp.float32)
        for block_id in range(block_total):

            def mix_fn(prob_bf=prob_bf_blocks[block_id], value_block=group_values[block_id]):
                return jnp.einsum(
                    "jts,sd->tjd", prob_bf, value_block, preferred_element_type=jnp.float32
                )

            attended_acc = attended_acc + mix_fn()
        attended_bf = attended_acc.astype(jnp.bfloat16)
        attended_cols.append(attended_bf.reshape(seq_rows, group_size * HD))
        attended_back = lax.optimization_barrier(attended_bf).astype(jnp.float32)
        delta_row = jnp.sum(grad_group.astype(jnp.float32) * attended_back, axis=-1)
        delta_col = jnp.transpose(delta_row)[:, :, None]
        query_acc = jnp.zeros((seq_rows, group_size, HD), jnp.float32)
        for block_id in range(block_total):

            def grad_fn(
                block_prob=prob_blocks[block_id],
                prob_bf=prob_bf_blocks[block_id],
                key_block=group_keys[block_id],
                value_block=group_values[block_id],
            ):
                dprobs = jnp.einsum(
                    "tjd,sd->jts", grad_group, value_block, preferred_element_type=jnp.float32
                )
                dscores = (block_prob * (dprobs - delta_col)).astype(jnp.bfloat16)
                query_term = (
                    jnp.einsum(
                        "jts,sd->tjd", dscores, key_block, preferred_element_type=jnp.float32
                    )
                    * scaling
                )
                key_term = (
                    jnp.einsum(
                        "jts,tjd->sd", dscores, query_group, preferred_element_type=jnp.float32
                    )
                    * scaling
                )
                value_term = jnp.einsum(
                    "jts,tjd->sd", prob_bf, grad_group, preferred_element_type=jnp.float32
                )
                return (query_term, key_term, value_term)

            query_term, key_term, value_term = grad_fn()
            query_acc = query_acc + query_term
            key_parts[block_id].append(key_term)
            value_parts[block_id].append(value_term)
        query_cols.append(query_acc.astype(jnp.bfloat16).reshape(seq_rows, group_size * HD))
    attended = jnp.concatenate(attended_cols, axis=1)
    query_grad = jnp.concatenate(query_cols, axis=1)
    key_cat = [jnp.concatenate(key_parts[index], axis=1) for index in range(block_total)]
    value_cat = [jnp.concatenate(value_parts[index], axis=1) for index in range(block_total)]
    key_total = key_cat[REACH]
    value_total = value_cat[REACH]
    for step in range(REACH):
        arrived = (
            from_behind(key_cat[step].astype(jnp.bfloat16), ("ctx", "rep"), step - REACH).astype(
                jnp.float32
            ),
            from_behind(value_cat[step].astype(jnp.bfloat16), ("ctx", "rep"), step - REACH).astype(
                jnp.float32
            ),
        )
        key_total = key_total + arrived[0]
        value_total = value_total + arrived[1]
    return (attended, query_grad, key_total.astype(jnp.bfloat16), value_total.astype(jnp.bfloat16))


def solution(mesh):
    in_specs = (
        P(("ctx", "rep"), "tp"),
        P(("ctx", "rep"), "tp"),
        P(("ctx", "rep"), "tp"),
        P(("ctx", "rep"), "tp"),
        P(),
    )
    out_specs = (
        P(("ctx", "rep"), "tp"),
        P(("ctx", "rep"), "tp"),
        P(("ctx", "rep"), "tp"),
        P(("ctx", "rep"), "tp"),
    )
    return jax.shard_map(
        per_device, mesh=mesh, in_specs=in_specs, out_specs=out_specs, check_vma=False
    )
```

profile of v0, /device:TPU:121, one launch (start us, length us, event | category | flops | bytes accessed | tf_op | source)
XLA Modules:
  0.0 88.7 jit_solution(4865337141845554902)
XLA Ops:
  0.6 3.1 %collective-permute-start.3 = (bf16[192,256]{1,0:T(8,128)(2,1)}, bf16[192,256]{1,0:T(8,128)(2,1)S(1)}, u32[]{:S(2)}, u32[]{:S(2)}) collective-permute-start(bf16[192,256]{1,0:T(8,128)(2,1)} %param.6), channel_id=1, source_target_pairs={{0,1},{1,2},{2,3},{3,16},{16,17},{17,18},{18,19},{19,32},{32,33},{... | collective-permute-start | bytes 294920 | tf_op jit(solution)/shard_map/ppermute | solution.py:18
  3.8 4.4 %collective-permute-start.2 = (bf16[192,256]{1,0:T(8,128)(2,1)}, bf16[192,256]{1,0:T(8,128)(2,1)S(1)}, u32[]{:S(2)}, u32[]{:S(2)}) collective-permute-start(bf16[192,256]{1,0:T(8,128)(2,1)} %param.6), channel_id=1, source_target_pairs={{0,2},{1,3},{2,16},{3,17},{16,18},{17,19},{18,32},{19,33},{32,34},... | collective-permute-start | bytes 294920 | tf_op jit(solution)/shard_map/ppermute | solution.py:18
  8.1 6.1 %collective-permute-start.1 = (bf16[192,256]{1,0:T(8,128)(2,1)}, bf16[192,256]{1,0:T(8,128)(2,1)S(1)}, u32[]{:S(2)}, u32[]{:S(2)}) collective-permute-start(bf16[192,256]{1,0:T(8,128)(2,1)} %param.6), channel_id=1, source_target_pairs={{0,3},{1,16},{2,17},{3,18},{16,19},{17,32},{18,33},{19,34},{32,35}... | collective-permute-start | bytes 294920 | tf_op jit(solution)/shard_map/ppermute | solution.py:18
  14.3 1.9 %collective-permute-start = (bf16[192,256]{1,0:T(8,128)(2,1)}, bf16[192,256]{1,0:T(8,128)(2,1)S(1)}, u32[]{:S(2)}, u32[]{:S(2)}) collective-permute-start(bf16[192,256]{1,0:T(8,128)(2,1)} %param.6), channel_id=1, source_target_pairs={{0,16},{1,17},{2,18},{3,19},{16,32},{17,33},{18,34},{19,35},{32,48... | collective-permute-start | bytes 294920 | tf_op jit(solution)/shard_map/ppermute | solution.py:18
  16.2 2.5 %collective-permute-start.7 = (bf16[192,256]{1,0:T(8,128)(2,1)}, bf16[192,256]{1,0:T(8,128)(2,1)S(1)}, u32[]{:S(2)}, u32[]{:S(2)}) collective-permute-start(bf16[192,256]{1,0:T(8,128)(2,1)} %param.7), channel_id=1, source_target_pairs={{0,1},{1,2},{2,3},{3,16},{16,17},{17,18},{18,19},{19,32},{32,33},{... | collective-permute-start | bytes 294920 | tf_op jit(solution)/shard_map/ppermute | solution.py:18
  18.8 0.7 copy-done.3
  20.1 1.0 %slice_bitcast_fusion.3 = (bf16[24,4,8,128]{3,2,1,0:T(8,128)(2,1)S(1)}, bf16[24,4,8,128]{3,2,1,0:T(8,128)(2,1)S(1)}) fusion(bf16[192,1024]{1,0:T(8,128)(2,1)} %param.5), kind=kLoop, calls=%fused_computation.234 | loop fusion | bytes 786432
  21.1 0.4 convert_reduce_fusion.2
  21.6 0.6 and_and_fusion.3
  23.1 0.7 copy-done.2
  23.8 0.8 copy-done
  24.7 3.7 %collective-permute-start.6 = (bf16[192,256]{1,0:T(8,128)(2,1)S(1)}, bf16[192,256]{1,0:T(8,128)(2,1)S(1)}, u32[]{:S(2)}, u32[]{:S(2)}) collective-permute-start(bf16[192,256]{1,0:T(8,128)(2,1)S(1)} %copy-done), channel_id=1, source_target_pairs={{0,2},{1,3},{2,16},{3,17},{16,18},{17,19},{18,32},{19,33},{32,34},... | collective-permute-start | bytes 294920 | tf_op jit(solution)/shard_map/ppermute | solution.py:18
  28.7 3.9 %collective-permute-start.5 = (bf16[192,256]{1,0:T(8,128)(2,1)S(1)}, bf16[192,256]{1,0:T(8,128)(2,1)S(1)}, u32[]{:S(2)}, u32[]{:S(2)}) collective-permute-start(bf16[192,256]{1,0:T(8,128)(2,1)S(1)} %copy-done), channel_id=1, source_target_pairs={{0,3},{1,16},{2,17},{3,18},{16,19},{17,32},{18,33},{19,34},{32,35}... | collective-permute-start | bytes 294920 | tf_op jit(solution)/shard_map/ppermute | solution.py:18
  32.9 3.1 %collective-permute-start.4 = (bf16[192,256]{1,0:T(8,128)(2,1)S(1)}, bf16[192,256]{1,0:T(8,128)(2,1)S(1)}, u32[]{:S(2)}, u32[]{:S(2)}) collective-permute-start(bf16[192,256]{1,0:T(8,128)(2,1)S(1)} %copy-done), channel_id=1, source_target_pairs={{0,16},{1,17},{2,18},{3,19},{16,32},{17,33},{18,34},{19,35},{32,48... | collective-permute-start | bytes 294920 | tf_op jit(solution)/shard_map/ppermute | solution.py:18
  36.7 0.6 exponential_reduce_fusion.8
  43.0 0.6 exponential_reduce_fusion.3
  46.6 0.3 fusion.64
  51.4 0.5 fusion.68
  52.0 2.9 %collective-permute-start.15 = (bf16[192,256]{1,0:T(8,128)(2,1)S(1)}, bf16[192,256]{1,0:T(8,128)(2,1)S(1)}, u32[]{:S(2)}, u32[]{:S(2)}) collective-permute-start(bf16[192,256]{1,0:T(8,128)(2,1)S(1)} %pad_maximum_fusion.9), channel_id=1, source_target_pairs={{1,0},{2,1},{3,2},{16,3},{17,16},{18,17},{19,18},{32,19},{33,32},{... | collective-permute-start | bytes 294920 | tf_op jit(solution)/shard_map/ppermute | solution.py:18
  54.9 2.6 %collective-permute-start.14 = (bf16[192,256]{1,0:T(8,128)(2,1)S(1)}, bf16[192,256]{1,0:T(8,128)(2,1)S(1)}, u32[]{:S(2)}, u32[]{:S(2)}) collective-permute-start(bf16[192,256]{1,0:T(8,128)(2,1)S(1)} %pad_maximum_fusion.8), channel_id=1, source_target_pairs={{2,0},{3,1},{16,2},{17,3},{18,16},{19,17},{32,18},{33,19},{34,32},... | collective-permute-start | bytes 294920 | tf_op jit(solution)/shard_map/ppermute | solution.py:18
  57.6 3.8 %collective-permute-start.13 = (bf16[192,256]{1,0:T(8,128)(2,1)S(1)}, bf16[192,256]{1,0:T(8,128)(2,1)S(1)}, u32[]{:S(2)}, u32[]{:S(2)}) collective-permute-start(bf16[192,256]{1,0:T(8,128)(2,1)S(1)} %pad_maximum_fusion.7), channel_id=1, source_target_pairs={{3,0},{16,1},{17,2},{18,3},{19,16},{32,17},{33,18},{34,19},{35,32}... | collective-permute-start | bytes 294920 | tf_op jit(solution)/shard_map/ppermute | solution.py:18
  61.4 1.9 %collective-permute-start.12 = (bf16[192,256]{1,0:T(8,128)(2,1)S(1)}, bf16[192,256]{1,0:T(8,128)(2,1)S(1)}, u32[]{:S(2)}, u32[]{:S(2)}) collective-permute-start(bf16[192,256]{1,0:T(8,128)(2,1)S(1)} %pad_maximum_fusion.6), channel_id=1, source_target_pairs={{16,0},{17,1},{18,2},{19,3},{32,16},{33,17},{34,18},{35,19},{48,32... | collective-permute-start | bytes 294920 | tf_op jit(solution)/shard_map/ppermute | solution.py:18
  67.1 3.5 %collective-permute-start.9 = (bf16[192,256]{1,0:T(8,128)(2,1)S(1)}, bf16[192,256]{1,0:T(8,128)(2,1)S(1)}, u32[]{:S(2)}, u32[]{:S(2)}) collective-permute-start(bf16[192,256]{1,0:T(8,128)(2,1)S(1)} %pad_maximum_fusion.3), channel_id=1, source_target_pairs={{3,0},{16,1},{17,2},{18,3},{19,16},{32,17},{33,18},{34,19},{35,32}... | collective-permute-start | bytes 294920 | tf_op jit(solution)/shard_map/ppermute | solution.py:18
  70.6 0.8 pad_maximum_fusion.1
  71.4 0.8 pad_maximum_fusion
  72.2 3.9 %collective-permute-start.10 = (bf16[192,256]{1,0:T(8,128)(2,1)S(1)}, bf16[192,256]{1,0:T(8,128)(2,1)S(1)}, u32[]{:S(2)}, u32[]{:S(2)}) collective-permute-start(bf16[192,256]{1,0:T(8,128)(2,1)S(1)} %pad_maximum_fusion.4), channel_id=1, source_target_pairs={{2,0},{3,1},{16,2},{17,3},{18,16},{19,17},{32,18},{33,19},{34,32},... | collective-permute-start | bytes 294920 | tf_op jit(solution)/shard_map/ppermute | solution.py:18
  76.1 2.6 %collective-permute-start.11 = (bf16[192,256]{1,0:T(8,128)(2,1)S(1)}, bf16[192,256]{1,0:T(8,128)(2,1)S(1)}, u32[]{:S(2)}, u32[]{:S(2)}) collective-permute-start(bf16[192,256]{1,0:T(8,128)(2,1)S(1)} %pad_maximum_fusion.5), channel_id=1, source_target_pairs={{1,0},{2,1},{3,2},{16,3},{17,16},{18,17},{19,18},{32,19},{33,32},{... | collective-permute-start | bytes 294920 | tf_op jit(solution)/shard_map/ppermute | solution.py:18
  78.8 1.9 %collective-permute-start.8 = (bf16[192,256]{1,0:T(8,128)(2,1)S(1)}, bf16[192,256]{1,0:T(8,128)(2,1)S(1)}, u32[]{:S(2)}, u32[]{:S(2)}) collective-permute-start(bf16[192,256]{1,0:T(8,128)(2,1)S(1)} %pad_maximum_fusion.2), channel_id=1, source_target_pairs={{16,0},{17,1},{18,2},{19,3},{32,16},{33,17},{34,18},{35,19},{48,32... | collective-permute-start | bytes 294920 | tf_op jit(solution)/shard_map/ppermute | solution.py:18
  80.7 0.7 fusion.153
  81.4 1.0 %collective-permute-done.11 = bf16[192,256]{1,0:T(8,128)(2,1)S(1)} collective-permute-done((bf16[192,256]{1,0:T(8,128)(2,1)S(1)}, bf16[192,256]{1,0:T(8,128)(2,1)S(1)}, u32[]{:S(2)}, u32[]{:S(2)}) %collective-permute-start.11) | collective-permute-done | bytes 98336 | tf_op jit(solution)/shard_map/ppermute | solution.py:18
  82.4 5.6 %collective-permute-done.8 = bf16[192,256]{1,0:T(8,128)(2,1)S(1)} collective-permute-done((bf16[192,256]{1,0:T(8,128)(2,1)S(1)}, bf16[192,256]{1,0:T(8,128)(2,1)S(1)}, u32[]{:S(2)}, u32[]{:S(2)}) %collective-permute-start.8) | collective-permute-done | bytes 98336 | tf_op jit(solution)/shard_map/ppermute | solution.py:18
  88.0 0.7 fusion.149
  (108 shorter events, 19.4 us)
Async XLA Ops:
  0.6 23.2 %collective-permute-start.3 = (bf16[192,256]{1,0:T(8,128)(2,1)}, bf16[192,256]{1,0:T(8,128)(2,1)S(1)}, u32[]{:S(2)}, u32[]{:S(2)}) collective-permute-start(bf16[192,256]{1,0:T(8,128)(2,1)} %param.6), channel_id=1, source_target_pairs={{0,1},{1,2},{2,3},{3,16},{16,17},{17,18},{18,19},{19,32},{32,33},{... | collective-permute-start | bytes 294920 | tf_op jit(solution)/shard_map/ppermute | solution.py:18
  3.8 24.9 %collective-permute-start.2 = (bf16[192,256]{1,0:T(8,128)(2,1)}, bf16[192,256]{1,0:T(8,128)(2,1)S(1)}, u32[]{:S(2)}, u32[]{:S(2)}) collective-permute-start(bf16[192,256]{1,0:T(8,128)(2,1)} %param.6), channel_id=1, source_target_pairs={{0,2},{1,3},{2,16},{3,17},{16,18},{17,19},{18,32},{19,33},{32,34},... | collective-permute-start | bytes 294920 | tf_op jit(solution)/shard_map/ppermute | solution.py:18
  8.1 24.8 %collective-permute-start.1 = (bf16[192,256]{1,0:T(8,128)(2,1)}, bf16[192,256]{1,0:T(8,128)(2,1)S(1)}, u32[]{:S(2)}, u32[]{:S(2)}) collective-permute-start(bf16[192,256]{1,0:T(8,128)(2,1)} %param.6), channel_id=1, source_target_pairs={{0,3},{1,16},{2,17},{3,18},{16,19},{17,32},{18,33},{19,34},{32,35}... | collective-permute-start | bytes 294920 | tf_op jit(solution)/shard_map/ppermute | solution.py:18
  14.3 22.1 %collective-permute-start = (bf16[192,256]{1,0:T(8,128)(2,1)}, bf16[192,256]{1,0:T(8,128)(2,1)S(1)}, u32[]{:S(2)}, u32[]{:S(2)}) collective-permute-start(bf16[192,256]{1,0:T(8,128)(2,1)} %param.6), channel_id=1, source_target_pairs={{0,16},{1,17},{2,18},{3,19},{16,32},{17,33},{18,34},{19,35},{32,48... | collective-permute-start | bytes 294920 | tf_op jit(solution)/shard_map/ppermute | solution.py:18
  16.2 23.4 %collective-permute-start.7 = (bf16[192,256]{1,0:T(8,128)(2,1)}, bf16[192,256]{1,0:T(8,128)(2,1)S(1)}, u32[]{:S(2)}, u32[]{:S(2)}) collective-permute-start(bf16[192,256]{1,0:T(8,128)(2,1)} %param.7), channel_id=1, source_target_pairs={{0,1},{1,2},{2,3},{3,16},{16,17},{17,18},{18,19},{19,32},{32,33},{... | collective-permute-start | bytes 294920 | tf_op jit(solution)/shard_map/ppermute | solution.py:18
  18.8 0.7 copy-start.3
  21.6 0.9 %copy-start.1 = (bf16[192,256]{1,0:T(8,128)(2,1)S(1)}, bf16[192,256]{1,0:T(8,128)(2,1)}, u32[]{:S(2)}) copy-start(bf16[192,256]{1,0:T(8,128)(2,1)} %param.6) | copy-start | bytes 294916
  22.8 1.0 %copy-start.2 = (bf16[192,1024]{1,0:T(8,128)(2,1)S(1)}, bf16[192,1024]{1,0:T(8,128)(2,1)}, u32[]{:S(2)}) copy-start(bf16[192,1024]{1,0:T(8,128)(2,1)} %param.8) | copy-start | bytes 1179652
  23.8 0.9 %copy-start = (bf16[192,256]{1,0:T(8,128)(2,1)S(1)}, bf16[192,256]{1,0:T(8,128)(2,1)}, u32[]{:S(2)}) copy-start(bf16[192,256]{1,0:T(8,128)(2,1)} %param.7) | copy-start | bytes 294916
  24.7 14.3 %collective-permute-start.6 = (bf16[192,256]{1,0:T(8,128)(2,1)S(1)}, bf16[192,256]{1,0:T(8,128)(2,1)S(1)}, u32[]{:S(2)}, u32[]{:S(2)}) collective-permute-start(bf16[192,256]{1,0:T(8,128)(2,1)S(1)} %copy-done), channel_id=1, source_target_pairs={{0,2},{1,3},{2,16},{3,17},{16,18},{17,19},{18,32},{19,33},{32,34},... | collective-permute-start | bytes 294920 | tf_op jit(solution)/shard_map/ppermute | solution.py:18
  28.7 9.6 %collective-permute-start.5 = (bf16[192,256]{1,0:T(8,128)(2,1)S(1)}, bf16[192,256]{1,0:T(8,128)(2,1)S(1)}, u32[]{:S(2)}, u32[]{:S(2)}) collective-permute-start(bf16[192,256]{1,0:T(8,128)(2,1)S(1)} %copy-done), channel_id=1, source_target_pairs={{0,3},{1,16},{2,17},{3,18},{16,19},{17,32},{18,33},{19,34},{32,35}... | collective-permute-start | bytes 294920 | tf_op jit(solution)/shard_map/ppermute | solution.py:18
  32.9 7.3 %collective-permute-start.4 = (bf16[192,256]{1,0:T(8,128)(2,1)S(1)}, bf16[192,256]{1,0:T(8,128)(2,1)S(1)}, u32[]{:S(2)}, u32[]{:S(2)}) collective-permute-start(bf16[192,256]{1,0:T(8,128)(2,1)S(1)} %copy-done), channel_id=1, source_target_pairs={{0,16},{1,17},{2,18},{3,19},{16,32},{17,33},{18,34},{19,35},{32,48... | collective-permute-start | bytes 294920 | tf_op jit(solution)/shard_map/ppermute | solution.py:18
  52.0 20.2 %collective-permute-start.15 = (bf16[192,256]{1,0:T(8,128)(2,1)S(1)}, bf16[192,256]{1,0:T(8,128)(2,1)S(1)}, u32[]{:S(2)}, u32[]{:S(2)}) collective-permute-start(bf16[192,256]{1,0:T(8,128)(2,1)S(1)} %pad_maximum_fusion.9), channel_id=1, source_target_pairs={{1,0},{2,1},{3,2},{16,3},{17,16},{18,17},{19,18},{32,19},{33,32},{... | collective-permute-start | bytes 294920 | tf_op jit(solution)/shard_map/ppermute | solution.py:18
  54.9 21.2 %collective-permute-start.14 = (bf16[192,256]{1,0:T(8,128)(2,1)S(1)}, bf16[192,256]{1,0:T(8,128)(2,1)S(1)}, u32[]{:S(2)}, u32[]{:S(2)}) collective-permute-start(bf16[192,256]{1,0:T(8,128)(2,1)S(1)} %pad_maximum_fusion.8), channel_id=1, source_target_pairs={{2,0},{3,1},{16,2},{17,3},{18,16},{19,17},{32,18},{33,19},{34,32},... | collective-permute-start | bytes 294920 | tf_op jit(solution)/shard_map/ppermute | solution.py:18
  57.6 21.2 %collective-permute-start.13 = (bf16[192,256]{1,0:T(8,128)(2,1)S(1)}, bf16[192,256]{1,0:T(8,128)(2,1)S(1)}, u32[]{:S(2)}, u32[]{:S(2)}) collective-permute-start(bf16[192,256]{1,0:T(8,128)(2,1)S(1)} %pad_maximum_fusion.7), channel_id=1, source_target_pairs={{3,0},{16,1},{17,2},{18,3},{19,16},{32,17},{33,18},{34,19},{35,32}... | collective-permute-start | bytes 294920 | tf_op jit(solution)/shard_map/ppermute | solution.py:18
  61.4 19.3 %collective-permute-start.12 = (bf16[192,256]{1,0:T(8,128)(2,1)S(1)}, bf16[192,256]{1,0:T(8,128)(2,1)S(1)}, u32[]{:S(2)}, u32[]{:S(2)}) collective-permute-start(bf16[192,256]{1,0:T(8,128)(2,1)S(1)} %pad_maximum_fusion.6), channel_id=1, source_target_pairs={{16,0},{17,1},{18,2},{19,3},{32,16},{33,17},{34,18},{35,19},{48,32... | collective-permute-start | bytes 294920 | tf_op jit(solution)/shard_map/ppermute | solution.py:18
  67.1 14.3 %collective-permute-start.9 = (bf16[192,256]{1,0:T(8,128)(2,1)S(1)}, bf16[192,256]{1,0:T(8,128)(2,1)S(1)}, u32[]{:S(2)}, u32[]{:S(2)}) collective-permute-start(bf16[192,256]{1,0:T(8,128)(2,1)S(1)} %pad_maximum_fusion.3), channel_id=1, source_target_pairs={{3,0},{16,1},{17,2},{18,3},{19,16},{32,17},{33,18},{34,19},{35,32}... | collective-permute-start | bytes 294920 | tf_op jit(solution)/shard_map/ppermute | solution.py:18
  72.2 9.2 %collective-permute-start.10 = (bf16[192,256]{1,0:T(8,128)(2,1)S(1)}, bf16[192,256]{1,0:T(8,128)(2,1)S(1)}, u32[]{:S(2)}, u32[]{:S(2)}) collective-permute-start(bf16[192,256]{1,0:T(8,128)(2,1)S(1)} %pad_maximum_fusion.4), channel_id=1, source_target_pairs={{2,0},{3,1},{16,2},{17,3},{18,16},{19,17},{32,18},{33,19},{34,32},... | collective-permute-start | bytes 294920 | tf_op jit(solution)/shard_map/ppermute | solution.py:18
  76.1 6.3 %collective-permute-start.11 = (bf16[192,256]{1,0:T(8,128)(2,1)S(1)}, bf16[192,256]{1,0:T(8,128)(2,1)S(1)}, u32[]{:S(2)}, u32[]{:S(2)}) collective-permute-start(bf16[192,256]{1,0:T(8,128)(2,1)S(1)} %pad_maximum_fusion.5), channel_id=1, source_target_pairs={{1,0},{2,1},{3,2},{16,3},{17,16},{18,17},{19,18},{32,19},{33,32},{... | collective-permute-start | bytes 294920 | tf_op jit(solution)/shard_map/ppermute | solution.py:18
  78.8 9.3 %collective-permute-start.8 = (bf16[192,256]{1,0:T(8,128)(2,1)S(1)}, bf16[192,256]{1,0:T(8,128)(2,1)S(1)}, u32[]{:S(2)}, u32[]{:S(2)}) collective-permute-start(bf16[192,256]{1,0:T(8,128)(2,1)S(1)} %pad_maximum_fusion.2), channel_id=1, source_target_pairs={{16,0},{17,1},{18,2},{19,3},{32,16},{33,17},{34,18},{35,19},{48,32... | collective-permute-start | bytes 294920 | tf_op jit(solution)/shard_map/ppermute | solution.py:18
where the time goes:
time: 89.4 us; the launch traced here: 88.7 us
  starting transfers between devices  51.9 us (58%)
  matrix products  18.5 us (21%)
  waiting for transfers between devices  6.64 us (7%)
  other arithmetic  6.36 us (7%)
  local copies, waits for them, and re-layouts  3.86 us (4%)
  between operations  1.42 us (2%)
    ppermute x16, starting transfers between devices, from_behind(): return lax.ppermute(block, axis, route)  51.9 us
    ppermute x16, waiting for transfers between devices, from_behind(): return lax.ppermute(block, axis, route)  6.64 us
    unnamed x10, local copies, waits for them, and re-layouts  3.54 us
    dot_general x10, matrix products, grad_fn(): jnp.einsum('jts,sd->tjd', dscores, key_block, preferred_element_type=jnp....  3.39 us
    dot_general x10, matrix products, mix_fn(): jnp.einsum('jts,sd->tjd', prob_bf, value_block, preferred_element_type=jn...  3.3 us
    dot_general x10, matrix products, score_fn(): jnp.einsum('tjd,sd->jts', query_group, key_block, preferred_element_type=...  3.08 us
    dot_general x10, matrix products, grad_fn(): jnp.einsum('jts,tjd->sd', prob_bf, grad_group, preferred_element_type=jnp...  2.97 us
    dot_general x10, matrix products, grad_fn(): jnp.einsum('tjd,sd->jts', grad_group, value_block, preferred_element_type...  2.91 us
  transfers between devices with their start and end apart: 16, of which 2 were waited for; matrix products, arithmetic and copies ran while one was open for 16% of the time, Pallas kernels for 0%

commit v1 on v0

v1 whole, which is shorter than its diff:
```python
import math

import jax
import jax.numpy as jnp
from jax import lax
from jax.experimental import pallas as pl
from jax.experimental.pallas import tpu as pltpu
from jax.sharding import PartitionSpec as P

HD = 128
REACH = 4
MASKED = -1e30
SCALING = 1.0 / math.sqrt(HD)
EXP2_SCALING = SCALING * math.log2(math.e)


def shifted(block, distance):
    axes = ("ctx", "rep")
    devices = range(lax.axis_size(axes))
    route = [(i, i + distance) for i in devices if i + distance in devices]
    return lax.ppermute(block, axes, route)


def contract(a, b, dim_a, dim_b):
    return lax.dot_general(
        a, b, (((dim_a,), (dim_b,)), ((), ())), preferred_element_type=jnp.float32
    )


def attention_kernel(first_ref, lengths_ref, q_ref, g_ref, *refs):
    blocks = REACH + 1
    kv_refs, refs = refs[:blocks], refs[blocks:]
    att_ref, qg_ref, own_ref = refs[:3]
    term_refs = refs[3 : 3 + REACH]
    p_scr, ds_scr = refs[3 + REACH :]
    rows = q_ref.shape[0]
    kv_heads = kv_refs[0].shape[1] // (2 * HD)
    group = q_ref.shape[1] // HD // kv_heads
    keys = blocks * rows
    pair = 2
    cols = pair * rows

    lengths = lengths_ref[...]
    docs = lengths.shape[1]
    upto = lax.broadcasted_iota(jnp.int32, (docs, docs), 1) <= lax.broadcasted_iota(
        jnp.int32, (docs, docs), 0
    )
    ends = jnp.sum(jnp.where(upto, lengths, 0), axis=1, keepdims=True)
    first = first_ref[0]
    pos = first + lax.broadcasted_iota(jnp.int32, (docs, rows), 1)
    begins = jnp.max(jnp.where(ends <= pos, ends, 0), axis=0, keepdims=True)
    low = begins - first + REACH * rows
    high = REACH * rows + lax.broadcasted_iota(jnp.int32, (1, rows), 1)
    low = jnp.concatenate([low] * pair, axis=1)
    high = jnp.concatenate([high] * pair, axis=1)
    key = lax.broadcasted_iota(jnp.int32, (keys, cols), 0)
    allowed = (key >= low) & (key <= high)

    for kv in range(kv_heads):
        k_cols = slice(kv * HD, (kv + 1) * HD)
        v_cols = slice((kv_heads + kv) * HD, (kv_heads + kv + 1) * HD)
        k = jnp.concatenate([r[:, k_cols] for r in kv_refs], axis=0)
        v = jnp.concatenate([r[:, v_cols] for r in kv_refs], axis=0)
        for part in range(group // pair):
            heads = [kv * group + part * pair + h for h in range(pair)]
            q = jnp.concatenate([q_ref[:, h * HD : (h + 1) * HD] for h in heads], axis=0)
            g = jnp.concatenate([g_ref[:, h * HD : (h + 1) * HD] for h in heads], axis=0)
            s = jnp.where(allowed, contract(k, q, 1, 1), MASKED)
            top = jnp.max(s, axis=0, keepdims=True)
            p = jnp.exp2((s - top) * EXP2_SCALING)
            p = p * (1.0 / jnp.sum(p, axis=0, keepdims=True))
            p_bf = p.astype(jnp.bfloat16)
            att = contract(v, p_bf, 0, 0).astype(jnp.bfloat16)
            delta = jnp.sum(
                g.T.astype(jnp.float32) * att.astype(jnp.float32), axis=0, keepdims=True
            )
            ds = (p * (contract(v, g, 1, 1) - delta)).astype(jnp.bfloat16)
            qg = (contract(k, ds, 0, 0) * SCALING).astype(jnp.bfloat16)
            att_t = att.T
            qg_t = qg.T
            for n, h in enumerate(heads):
                att_ref[:, h * HD : (h + 1) * HD] = att_t[n * rows : (n + 1) * rows]
                qg_ref[:, h * HD : (h + 1) * HD] = qg_t[n * rows : (n + 1) * rows]
            p_scr[:, part * cols : (part + 1) * cols] = p_bf
            ds_scr[:, part * cols : (part + 1) * cols] = ds
        heads = [kv * group + h for h in range(group)]
        q = jnp.concatenate([q_ref[:, h * HD : (h + 1) * HD] for h in heads], axis=0)
        g = jnp.concatenate([g_ref[:, h * HD : (h + 1) * HD] for h in heads], axis=0)
        kg = contract(ds_scr[...], q, 1, 0) * SCALING
        vg = contract(p_scr[...], g, 1, 0)
        for n in range(REACH):
            term_refs[n][:, k_cols] = kg[n * rows : (n + 1) * rows].astype(jnp.bfloat16)
            term_refs[n][:, v_cols] = vg[n * rows : (n + 1) * rows].astype(jnp.bfloat16)
        own_ref[:, k_cols] = kg[REACH * rows :]
        own_ref[:, v_cols] = vg[REACH * rows :]


def attention(first, lengths, queries, out_grad, kv_blocks):
    rows, width = queries.shape
    kv_width = kv_blocks[0].shape[1]
    keys = (REACH + 1) * rows
    group_cols = rows * (width // HD) // (kv_width // (2 * HD))
    vmem = pl.BlockSpec(memory_space=pltpu.VMEM)
    term = jax.ShapeDtypeStruct((rows, kv_width), jnp.bfloat16)
    wide = jax.ShapeDtypeStruct((rows, width), jnp.bfloat16)
    flops = 6 * 2 * keys * rows * width
    return pl.pallas_call(
        attention_kernel,
        out_shape=(wide, wide, jax.ShapeDtypeStruct((rows, kv_width), jnp.float32))
        + (term,) * REACH,
        in_specs=[pl.BlockSpec(memory_space=pltpu.SMEM)] + [vmem] * (3 + REACH + 1),
        out_specs=(vmem,) * (3 + REACH),
        scratch_shapes=[
            pltpu.VMEM((keys, group_cols), jnp.bfloat16),
            pltpu.VMEM((keys, group_cols), jnp.bfloat16),
        ],
        compiler_params=pltpu.CompilerParams(vmem_limit_bytes=40 << 20),
        cost_estimate=pl.CostEstimate(
            flops=flops,
            bytes_accessed=8 * rows * width + 24 * rows * kv_width,
            transcendentals=keys * rows * width // HD,
        ),
        name="attention",
    )(first, lengths, queries, out_grad, *kv_blocks)


def per_device(queries, key_states, value_states, out_grad, doc_lengths):
    rows = queries.shape[0]
    width = key_states.shape[1]
    first = (lax.axis_index(("ctx", "rep")) * rows).astype(jnp.int32).reshape(1)
    own = jnp.concatenate([key_states, value_states], axis=1)
    received = [shifted(own, distance) for distance in range(REACH, 0, -1)]
    attended, query_grad, own_terms, *terms = attention(
        first, doc_lengths.reshape(1, -1), queries, out_grad, received + [own]
    )
    total = own_terms
    for distance, term in zip(range(REACH, 0, -1), terms):
        total = total + shifted(term, -distance).astype(jnp.float32)
    total = total.astype(jnp.bfloat16)
    return attended, query_grad, total[:, :width], total[:, width:]


def solution(mesh):
    split = P(("ctx", "rep"), "tp")
    return jax.shard_map(
        per_device,
        mesh=mesh,
        in_specs=(split, split, split, split, P()),
        out_specs=(split, split, split, split),
        check_vma=False,
    )
```

time: 89.4 us -> 55.2 us (0.62)
  the two profiles are of different devices: /device:TPU:121 before, /device:TPU:643 now
where the time goes in v1:
time: 55.2 us; the launch traced here: 54.8 us
  starting transfers between devices  29.4 us (53%)
  waiting for transfers between devices  11.9 us (22%)
  Pallas kernels  8.37 us (15%)
  local copies, waits for them, and re-layouts  4.21 us (8%)
  between operations  0.75 us (1%)
    ppermute x8, starting transfers between devices, shifted(): return lax.ppermute(block, axes, route)  29.4 us
    ppermute x8, waiting for transfers between devices, shifted(): return lax.ppermute(block, axes, route)  11.9 us
    pallas_call x1, Pallas kernels, attention(): pl.pallas_call(attention_kernel, out_shape=(wide, wide, jax.ShapeDtypeStr...  8.37 us
    unnamed x7, local copies, waits for them, and re-layouts  2.62 us
  transfers between devices with their start and end apart: 8, of which 3 were waited for; matrix products, arithmetic and copies ran while one was open for 0% of the time, Pallas kernels for 0%

profile of v1, /device:TPU:643, one launch (start us, length us, event | category | flops | bytes accessed | tf_op | source)
XLA Modules:
  0.0 54.8 jit_solution(16107371060196502676)
XLA Ops:
  0.6 0.0 copy-start
  0.6 0.9 %constant_dynamic-update-slice_fusion.1 = bf16[192,512]{1,0:T(8,128)(2,1)S(1)} fusion(bf16[192,256]{1,0:T(8,128)(2,1)} %param.6), kind=kLoop, calls=%fused_computation.2 | loop fusion | bytes 196608
  1.6 0.9 %constant_dynamic-update-slice_fusion.refs_4_ = bf16[192,512]{1,0:T(8,128)(2,1)S(1)} fusion(bf16[192,512]{1,0:T(8,128)(2,1)S(1)} %constant_dynamic-update-slice_fusion.1, bf16[192,256]{1,0:T(8,128)(2,1)} %param.7), kind=kLoop, calls=%fused_computation.1 | loop fusion | bytes 196608 | tf_op jit(solution)/shard_map/concatenate | solution.py:131
  2.5 3.1 %collective-permute-start.3 = (bf16[192,512]{1,0:T(8,128)(2,1)S(1)}, bf16[192,512]{1,0:T(8,128)(2,1)S(1)}, u32[]{:S(2)}, u32[]{:S(2)}) collective-permute-start(bf16[192,512]{1,0:T(8,128)(2,1)S(1)} %constant_dynamic-update-slice_fusion.refs_4_), channel_id=1, source_target_pairs={{0,1},{1,2},{2,3},{3,16},{16,17},{17,18},{18,19},{19,32},{32,33},{... | collective-permute-start | bytes 589832 | tf_op jit(solution)/shard_map/ppermute | solution.py:21
  5.6 4.3 %collective-permute-start.2 = (bf16[192,512]{1,0:T(8,128)(2,1)S(1)}, bf16[192,512]{1,0:T(8,128)(2,1)S(1)}, u32[]{:S(2)}, u32[]{:S(2)}) collective-permute-start(bf16[192,512]{1,0:T(8,128)(2,1)S(1)} %constant_dynamic-update-slice_fusion.refs_4_), channel_id=1, source_target_pairs={{0,2},{1,3},{2,16},{3,17},{16,18},{17,19},{18,32},{19,33},{32,34},... | collective-permute-start | bytes 589832 | tf_op jit(solution)/shard_map/ppermute | solution.py:21
  9.9 4.3 %collective-permute-start.1 = (bf16[192,512]{1,0:T(8,128)(2,1)S(1)}, bf16[192,512]{1,0:T(8,128)(2,1)S(1)}, u32[]{:S(2)}, u32[]{:S(2)}) collective-permute-start(bf16[192,512]{1,0:T(8,128)(2,1)S(1)} %constant_dynamic-update-slice_fusion.refs_4_), channel_id=1, source_target_pairs={{0,3},{1,16},{2,17},{3,18},{16,19},{17,32},{18,33},{19,34},{32,35}... | collective-permute-start | bytes 589832 | tf_op jit(solution)/shard_map/ppermute | solution.py:21
  14.3 1.9 %collective-permute-start = (bf16[192,512]{1,0:T(8,128)(2,1)S(1)}, bf16[192,512]{1,0:T(8,128)(2,1)S(1)}, u32[]{:S(2)}, u32[]{:S(2)}) collective-permute-start(bf16[192,512]{1,0:T(8,128)(2,1)S(1)} %constant_dynamic-update-slice_fusion.refs_4_), channel_id=1, source_target_pairs={{0,16},{1,17},{2,18},{3,19},{16,32},{17,33},{18,34},{19,35},{32,48... | collective-permute-start | bytes 589832 | tf_op jit(solution)/shard_map/ppermute | solution.py:21
  16.2 0.0 collective-permute-done.3.refs_3_
  16.2 0.0 collective-permute-done.2.refs_2_
  16.2 4.2 %collective-permute-done.1.refs_1_ = bf16[192,512]{1,0:T(8,128)(2,1)S(1)} collective-permute-done((bf16[192,512]{1,0:T(8,128)(2,1)S(1)}, bf16[192,512]{1,0:T(8,128)(2,1)S(1)}, u32[]{:S(2)}, u32[]{:S(2)}) %collective-permute-start.1) | collective-permute-done | bytes 196640 | tf_op jit(solution)/shard_map/ppermute | solution.py:21
  20.4 0.0 collective-permute-done.refs_0_
  20.4 0.0 copy-start.2
  20.4 0.0 copy-done
  20.4 0.7 %copy-done.2 = s32[255]{0:T(256)S(1)} copy-done((s32[255]{0:T(256)S(1)}, s32[255]{0:T(256)}, u32[]{:S(2)}) %copy-start.2) | copy-done | bytes 1044
  21.1 0.0 copy-start.1
  21.1 1.0 %copy-done.1 = bf16[192,1024]{1,0:T(8,128)(2,1)S(1)} copy-done((bf16[192,1024]{1,0:T(8,128)(2,1)S(1)}, bf16[192,1024]{1,0:T(8,128)(2,1)}, u32[]{:S(2)}) %copy-start.1) | copy-done | bytes 393240
  22.1 8.4 %attention.1 = (bf16[192,1024]{1,0:T(8,128)(2,1)}, bf16[192,1024]{1,0:T(8,128)(2,1)}, f32[192,512]{1,0:T(8,128)S(1)}, bf16[192,512]{1,0:T(8,128)(2,1)S(1)}, bf16...) custom-call(s32[1]{0:T(128)} %bitcast.first_ref, s32[1,255]{1,0:T(1,128)S(1)} %bitcast.2, ...), custom_call_target="tpu_custom_call" | custom-call | flops 2264924160 | bytes 3932160 | tf_op jit(solution)/shard_map/attention/pallas_call | solution.py:107
  30.5 5.1 %collective-permute-start.4 = (bf16[192,512]{1,0:T(8,128)(2,1)S(1)}, bf16[192,512]{1,0:T(8,128)(2,1)S(1)}, u32[]{:S(2)}, u32[]{:S(2)}) collective-permute-start(bf16[192,512]{1,0:T(8,128)(2,1)S(1)} %get-tuple-element.14), channel_id=1, source_target_pairs={{16,0},{17,1},{18,2},{19,3},{32,16},{33,17},{34,18},{35,19},{48,32... | collective-permute-start | bytes 589832 | tf_op jit(solution)/shard_map/ppermute | solution.py:21
  35.6 4.1 %collective-permute-start.5 = (bf16[192,512]{1,0:T(8,128)(2,1)S(1)}, bf16[192,512]{1,0:T(8,128)(2,1)S(1)}, u32[]{:S(2)}, u32[]{:S(2)}) collective-permute-start(bf16[192,512]{1,0:T(8,128)(2,1)S(1)} %get-tuple-element.15), channel_id=1, source_target_pairs={{3,0},{16,1},{17,2},{18,3},{19,16},{32,17},{33,18},{34,19},{35,32}... | collective-permute-start | bytes 589832 | tf_op jit(solution)/shard_map/ppermute | solution.py:21
  39.7 3.0 %collective-permute-start.6 = (bf16[192,512]{1,0:T(8,128)(2,1)S(1)}, bf16[192,512]{1,0:T(8,128)(2,1)S(1)}, u32[]{:S(2)}, u32[]{:S(2)}) collective-permute-start(bf16[192,512]{1,0:T(8,128)(2,1)S(1)} %get-tuple-element.16), channel_id=1, source_target_pairs={{2,0},{3,1},{16,2},{17,3},{18,16},{19,17},{32,18},{33,19},{34,32},... | collective-permute-start | bytes 589832 | tf_op jit(solution)/shard_map/ppermute | solution.py:21
  42.7 3.5 %collective-permute-start.7 = (bf16[192,512]{1,0:T(8,128)(2,1)S(1)}, bf16[192,512]{1,0:T(8,128)(2,1)S(1)}, u32[]{:S(2)}, u32[]{:S(2)}) collective-permute-start(bf16[192,512]{1,0:T(8,128)(2,1)S(1)} %get-tuple-element.17), channel_id=1, source_target_pairs={{1,0},{2,1},{3,2},{16,3},{17,16},{18,17},{19,18},{32,19},{33,32},{... | collective-permute-start | bytes 589832 | tf_op jit(solution)/shard_map/ppermute | solution.py:21
  46.2 0.0 collective-permute-done.4
  46.2 0.0 collective-permute-done.5
  46.2 2.8 %collective-permute-done.6 = bf16[192,512]{1,0:T(8,128)(2,1)S(1)} collective-permute-done((bf16[192,512]{1,0:T(8,128)(2,1)S(1)}, bf16[192,512]{1,0:T(8,128)(2,1)S(1)}, u32[]{:S(2)}, u32[]{:S(2)}) %collective-permute-start.6) | collective-permute-done | bytes 196640 | tf_op jit(solution)/shard_map/ppermute | solution.py:21
  49.0 5.0 %collective-permute-done.7 = bf16[192,512]{1,0:T(8,128)(2,1)S(1)} collective-permute-done((bf16[192,512]{1,0:T(8,128)(2,1)S(1)}, bf16[192,512]{1,0:T(8,128)(2,1)S(1)}, u32[]{:S(2)}, u32[]{:S(2)}) %collective-permute-start.7) | collective-permute-done | bytes 196640 | tf_op jit(solution)/shard_map/ppermute | solution.py:21
  54.0 0.1 add_convert_fusion
  54.1 0.7 %fusion = (bf16[192,256]{1,0:T(8,128)(2,1)}, bf16[192,256]{1,0:T(8,128)(2,1)}) fusion(bf16[192,512]{1,0:T(8,128)(2,1)S(1)} %add_convert_fusion), kind=kLoop, calls=%fused_computation.3 | loop fusion | bytes 393216 | tf_op jit(solution)/shard_map/slice | solution.py:140
Async XLA Ops:
  0.6 19.8 %copy-start = (bf16[192,1024]{1,0:T(8,128)(2,1)S(1)}, bf16[192,1024]{1,0:T(8,128)(2,1)}, u32[]{:S(2)}) copy-start(bf16[192,1024]{1,0:T(8,128)(2,1)} %q_ref.1) | copy-start | bytes 1179652
  2.5 13.7 %collective-permute-start.3 = (bf16[192,512]{1,0:T(8,128)(2,1)S(1)}, bf16[192,512]{1,0:T(8,128)(2,1)S(1)}, u32[]{:S(2)}, u32[]{:S(2)}) collective-permute-start(bf16[192,512]{1,0:T(8,128)(2,1)S(1)} %constant_dynamic-update-slice_fusion.refs_4_), channel_id=1, source_target_pairs={{0,1},{1,2},{2,3},{3,16},{16,17},{17,18},{18,19},{19,32},{32,33},{... | collective-permute-start | bytes 589832 | tf_op jit(solution)/shard_map/ppermute | solution.py:21
  5.6 10.6 %collective-permute-start.2 = (bf16[192,512]{1,0:T(8,128)(2,1)S(1)}, bf16[192,512]{1,0:T(8,128)(2,1)S(1)}, u32[]{:S(2)}, u32[]{:S(2)}) collective-permute-start(bf16[192,512]{1,0:T(8,128)(2,1)S(1)} %constant_dynamic-update-slice_fusion.refs_4_), channel_id=1, source_target_pairs={{0,2},{1,3},{2,16},{3,17},{16,18},{17,19},{18,32},{19,33},{32,34},... | collective-permute-start | bytes 589832 | tf_op jit(solution)/shard_map/ppermute | solution.py:21
  9.9 10.5 %collective-permute-start.1 = (bf16[192,512]{1,0:T(8,128)(2,1)S(1)}, bf16[192,512]{1,0:T(8,128)(2,1)S(1)}, u32[]{:S(2)}, u32[]{:S(2)}) collective-permute-start(bf16[192,512]{1,0:T(8,128)(2,1)S(1)} %constant_dynamic-update-slice_fusion.refs_4_), channel_id=1, source_target_pairs={{0,3},{1,16},{2,17},{3,18},{16,19},{17,32},{18,33},{19,34},{32,35}... | collective-permute-start | bytes 589832 | tf_op jit(solution)/shard_map/ppermute | solution.py:21
  14.3 6.1 %collective-permute-start = (bf16[192,512]{1,0:T(8,128)(2,1)S(1)}, bf16[192,512]{1,0:T(8,128)(2,1)S(1)}, u32[]{:S(2)}, u32[]{:S(2)}) collective-permute-start(bf16[192,512]{1,0:T(8,128)(2,1)S(1)} %constant_dynamic-update-slice_fusion.refs_4_), channel_id=1, source_target_pairs={{0,16},{1,17},{2,18},{3,19},{16,32},{17,33},{18,34},{19,35},{32,48... | collective-permute-start | bytes 589832 | tf_op jit(solution)/shard_map/ppermute | solution.py:21
  20.4 0.7 %copy-start.2 = (s32[255]{0:T(256)S(1)}, s32[255]{0:T(256)}, u32[]{:S(2)}) copy-start(s32[255]{0:T(256)} %param.9) | copy-start | bytes 3064
  21.1 1.0 %copy-start.1 = (bf16[192,1024]{1,0:T(8,128)(2,1)S(1)}, bf16[192,1024]{1,0:T(8,128)(2,1)}, u32[]{:S(2)}) copy-start(bf16[192,1024]{1,0:T(8,128)(2,1)} %g_ref.1) | copy-start | bytes 1179652
  30.5 15.7 %collective-permute-start.4 = (bf16[192,512]{1,0:T(8,128)(2,1)S(1)}, bf16[192,512]{1,0:T(8,128)(2,1)S(1)}, u32[]{:S(2)}, u32[]{:S(2)}) collective-permute-start(bf16[192,512]{1,0:T(8,128)(2,1)S(1)} %get-tuple-element.14), channel_id=1, source_target_pairs={{16,0},{17,1},{18,2},{19,3},{32,16},{33,17},{34,18},{35,19},{48,32... | collective-permute-start | bytes 589832 | tf_op jit(solution)/shard_map/ppermute | solution.py:21
  35.6 10.6 %collective-permute-start.5 = (bf16[192,512]{1,0:T(8,128)(2,1)S(1)}, bf16[192,512]{1,0:T(8,128)(2,1)S(1)}, u32[]{:S(2)}, u32[]{:S(2)}) collective-permute-start(bf16[192,512]{1,0:T(8,128)(2,1)S(1)} %get-tuple-element.15), channel_id=1, source_target_pairs={{3,0},{16,1},{17,2},{18,3},{19,16},{32,17},{33,18},{34,19},{35,32}... | collective-permute-start | bytes 589832 | tf_op jit(solution)/shard_map/ppermute | solution.py:21
  39.7 9.3 %collective-permute-start.6 = (bf16[192,512]{1,0:T(8,128)(2,1)S(1)}, bf16[192,512]{1,0:T(8,128)(2,1)S(1)}, u32[]{:S(2)}, u32[]{:S(2)}) collective-permute-start(bf16[192,512]{1,0:T(8,128)(2,1)S(1)} %get-tuple-element.16), channel_id=1, source_target_pairs={{2,0},{3,1},{16,2},{17,3},{18,16},{19,17},{32,18},{33,19},{34,32},... | collective-permute-start | bytes 589832 | tf_op jit(solution)/shard_map/ppermute | solution.py:21
  42.7 11.3 %collective-permute-start.7 = (bf16[192,512]{1,0:T(8,128)(2,1)S(1)}, bf16[192,512]{1,0:T(8,128)(2,1)S(1)}, u32[]{:S(2)}, u32[]{:S(2)}) collective-permute-start(bf16[192,512]{1,0:T(8,128)(2,1)S(1)} %get-tuple-element.17), channel_id=1, source_target_pairs={{1,0},{2,1},{3,2},{16,3},{17,16},{18,17},{19,18},{32,19},{33,32},{... | collective-permute-start | bytes 589832 | tf_op jit(solution)/shard_map/ppermute | solution.py:21

commit v2 on v1

v2 whole, which is shorter than its diff:
```python
import math

import jax
import jax.numpy as jnp
from jax import lax
from jax.experimental import pallas as pl
from jax.experimental.pallas import tpu as pltpu
from jax.sharding import PartitionSpec as P

HD = 128
REACH = 4
NEAR = 2
HALVES = 2
MASKED = -1e30
SCALING = 1.0 / math.sqrt(HD)
EXP2_SCALING = SCALING * math.log2(math.e)
VMEM = pl.BlockSpec(memory_space=pltpu.VMEM)
HBM = pl.BlockSpec(memory_space=pltpu.MemorySpace.HBM)


def shifted(block, distance):
    axes = ("ctx", "rep")
    devices = range(lax.axis_size(axes))
    route = [(i, i + distance) for i in devices if i + distance in devices]
    return lax.ppermute(block, axes, route)


def contract(a, b, dim_a, dim_b):
    return lax.dot_general(
        a, b, (((dim_a,), (dim_b,)), ((), ())), preferred_element_type=jnp.float32
    )


def call(kernel, name, outs, specs, operands, flops, scratch=()):
    size = lambda a: math.prod(a.shape) * jnp.dtype(a.dtype).itemsize
    return pl.pallas_call(
        kernel,
        out_shape=tuple(outs),
        in_specs=specs,
        out_specs=(VMEM,) * len(outs),
        scratch_shapes=list(scratch),
        compiler_params=pltpu.CompilerParams(vmem_limit_bytes=24 << 20),
        cost_estimate=pl.CostEstimate(
            flops=flops,
            bytes_accessed=sum(map(size, (*operands, *outs))),
            transcendentals=0,
        ),
        name=name,
    )(*operands)


def tile_of(ref, heads, half):
    part = ref.shape[0] // HALVES
    return jnp.concatenate(
        [ref[half * part : (half + 1) * part, h * HD : (h + 1) * HD] for h in heads], axis=0
    )


def key_cols(kv):
    return slice(kv * HD, (kv + 1) * HD)


def value_cols(kv, kv_heads):
    return slice((kv_heads + kv) * HD, (kv_heads + kv + 1) * HD)


def load_kernel(
    first_ref, lengths_hbm, k_hbm, v_hbm, q_hbm, g_hbm, kv_ref, q_ref, g_ref, low_ref, lengths_ref, sems
):
    width = k_hbm.shape[1]
    copies = [
        pltpu.make_async_copy(src, dst, sems.at[n])
        for n, (src, dst) in enumerate(
            [
                (lengths_hbm, lengths_ref),
                (k_hbm, kv_ref.at[:, :width]),
                (v_hbm, kv_ref.at[:, width:]),
                (q_hbm, q_ref),
                (g_hbm, g_ref),
            ]
        )
    ]
    for copy in copies:
        copy.start()
    copies[0].wait()
    rows = q_ref.shape[0]
    lengths = lengths_ref[...]
    docs = lengths.shape[1]
    upto = lax.broadcasted_iota(jnp.int32, (docs, docs), 1) <= lax.broadcasted_iota(
        jnp.int32, (docs, docs), 0
    )
    ends = jnp.sum(jnp.where(upto, lengths, 0), axis=1, keepdims=True)
    first = first_ref[0]
    pos = first + lax.broadcasted_iota(jnp.int32, (docs, rows), 1)
    begins = jnp.max(jnp.where(ends <= pos, ends, 0), axis=0, keepdims=True)
    low = begins - first + REACH * rows
    part = rows // HALVES
    group = low_ref.shape[1] // part
    for half in range(HALVES):
        low_ref[half : half + 1] = jnp.concatenate(
            [low[:, half * part : (half + 1) * part]] * group, axis=1
        )
    for copy in copies[1:]:
        copy.wait()


def near_kernel(low_ref, q_ref, g_ref, *refs):
    kv_refs = refs[NEAR - 1 :: -1] + refs[NEAR : NEAR + 1]
    p_ref, d_ref, stat_ref = refs[NEAR + 1 :]
    rows = q_ref.shape[0]
    part = rows // HALVES
    kv_heads = kv_refs[0].shape[1] // (2 * HD)
    group = q_ref.shape[1] // HD // kv_heads
    cols = group * part
    before = NEAR * rows
    offset = (REACH - NEAR) * rows
    for kv in range(kv_heads):
        heads = range(kv * group, (kv + 1) * group)
        for half in range(HALVES):
            own = (half + 1) * part
            keys = before + own
            k = jnp.concatenate([r[:, key_cols(kv)] for r in kv_refs], axis=0)[:keys]
            v = jnp.concatenate([r[:, value_cols(kv, kv_heads)] for r in kv_refs], axis=0)[:keys]
            q = tile_of(q_ref, heads, half)
            g = tile_of(g_ref, heads, half)
            low = low_ref[half : half + 1]
            query = half * part + lax.broadcasted_iota(jnp.int32, (1, cols), 1) % part
            key = lax.broadcasted_iota(jnp.int32, (before, cols), 0) + offset
            own_key = lax.broadcasted_iota(jnp.int32, (own, cols), 0)
            allowed = jnp.concatenate(
                [key >= low, (own_key + REACH * rows >= low) & (own_key <= query)], axis=0
            )
            s = jnp.where(allowed, contract(k, q, 1, 1), MASKED)
            top = jnp.max(s, axis=0, keepdims=True)
            p = jnp.exp2((s - top) * EXP2_SCALING)
            tile = slice(half * cols, (half + 1) * cols)
            p_ref[kv, :keys, tile] = p
            d_ref[kv, :keys, tile] = contract(v, g, 1, 1)
            stat_ref[kv, 0:1, tile] = top
            stat_ref[kv, 1:2, tile] = jnp.sum(p, axis=0, keepdims=True)


def terms_kernel(low_ref, q_ref, g_ref, p_ref, d_ref, stat_ref, *refs):
    blocks = REACH + 1
    kv_refs, refs = refs[:blocks], refs[blocks:]
    term_refs, (att_ref, ds_ref, own_ref, p_scr) = refs[:REACH], refs[REACH:]
    rows = q_ref.shape[0]
    part = rows // HALVES
    kv_heads = kv_refs[0].shape[1] // (2 * HD)
    group = q_ref.shape[1] // HD // kv_heads
    cols = group * part
    far = REACH - NEAR
    split = far * rows
    for kv in range(kv_heads):
        heads = range(kv * group, (kv + 1) * group)
        k = jnp.concatenate([r[:, key_cols(kv)] for r in kv_refs[:far]], axis=0)
        v = jnp.concatenate([r[:, value_cols(kv, kv_heads)] for r in kv_refs], axis=0)
        qs, gs = [], []
        for half in range(HALVES):
            start = half * part
            stop = REACH * rows + (half + 1) * part
            q = tile_of(q_ref, heads, half)
            g = tile_of(g_ref, heads, half)
            qs.append(q)
            gs.append(g)
            tile = slice(half * cols, (half + 1) * cols)
            low = low_ref[half : half + 1]
            key = lax.broadcasted_iota(jnp.int32, (split - start, cols), 0) + start
            s = jnp.where(key >= low, contract(k[start:], q, 1, 1), MASKED)
            near_top = stat_ref[kv, 0:1, tile]
            top = jnp.maximum(near_top, jnp.max(s, axis=0, keepdims=True))
            p = jnp.exp2((s - top) * EXP2_SCALING)
            ratio = jnp.exp2((near_top - top) * EXP2_SCALING)
            total = ratio * stat_ref[kv, 1:2, tile] + jnp.sum(p, axis=0, keepdims=True)
            inverse = 1.0 / total
            p = p * inverse
            p_near = p_ref[kv, : stop - split, tile] * (ratio * inverse)
            p_bf = jnp.concatenate([p.astype(jnp.bfloat16), p_near.astype(jnp.bfloat16)], axis=0)
            att = contract(v[start:stop], p_bf, 0, 0).astype(jnp.bfloat16)
            delta = jnp.sum(
                g.T.astype(jnp.float32) * att.astype(jnp.float32), axis=0, keepdims=True
            )
            ds = p * (contract(v[start:split], g, 1, 1) - delta)
            ds_near = p_near * (d_ref[kv, : stop - split, tile] - delta)
            att_ref[kv, :, tile] = att
            p_scr[start:stop, tile] = p_bf
            ds_ref[kv, start:split, tile] = ds.astype(jnp.bfloat16)
            ds_ref[kv, split:stop, tile] = ds_near.astype(jnp.bfloat16)
            rest = slice(0, start) if half else slice(stop, blocks * rows)
            p_scr[rest, tile] = jnp.zeros((part, cols), jnp.bfloat16)
            ds_ref[kv, rest, tile] = jnp.zeros((part, cols), jnp.bfloat16)
        remote = REACH * rows
        kg = contract(ds_ref[kv, :remote], jnp.concatenate(qs, axis=0), 1, 0) * SCALING
        vg = contract(p_scr[:remote], jnp.concatenate(gs, axis=0), 1, 0)
        for n in range(REACH):
            block = slice(n * rows, (n + 1) * rows)
            term_refs[n][:, key_cols(kv)] = kg[block].astype(jnp.bfloat16)
            term_refs[n][:, value_cols(kv, kv_heads)] = vg[block].astype(jnp.bfloat16)
        own_ref[kv] = p_scr[remote:]


def own_kernel(q_ref, g_ref, att_ref, ds_ref, own_ref, *refs):
    kv_refs = refs[: REACH + 1]
    att_out, qg_out, total_ref = refs[REACH + 1 :]
    rows = q_ref.shape[0]
    part = rows // HALVES
    kv_heads = kv_refs[0].shape[1] // (2 * HD)
    group = q_ref.shape[1] // HD // kv_heads
    cols = group * part
    remote = REACH * rows
    for kv in range(kv_heads):
        heads = range(kv * group, (kv + 1) * group)
        k = jnp.concatenate([r[:, key_cols(kv)] for r in kv_refs], axis=0)
        q = jnp.concatenate([tile_of(q_ref, heads, half) for half in range(HALVES)], axis=0)
        g = jnp.concatenate([tile_of(g_ref, heads, half) for half in range(HALVES)], axis=0)
        total_ref[:, key_cols(kv)] = contract(ds_ref[kv, remote:], q, 1, 0) * SCALING
        total_ref[:, value_cols(kv, kv_heads)] = contract(own_ref[kv], g, 1, 0)
        for half in range(HALVES):
            tile = slice(half * cols, (half + 1) * cols)
            start = half * part
            stop = remote + (half + 1) * part
            qg = contract(k[start:stop], ds_ref[kv, start:stop, tile], 0, 0) * SCALING
            qg = qg.astype(jnp.bfloat16).T
            att = att_ref[kv, :, tile].T
            for n, h in enumerate(heads):
                out = (slice(start, start + part), slice(h * HD, (h + 1) * HD))
                att_out[out] = att[n * part : (n + 1) * part]
                qg_out[out] = qg[n * part : (n + 1) * part]


def add_kernel(total_ref, *refs):
    term_refs, (k_ref, v_ref) = refs[:REACH], refs[REACH:]
    width = k_ref.shape[1]
    total = total_ref[...]
    for term_ref in term_refs:
        total = total + term_ref[...].astype(jnp.float32)
    k_ref[...] = total[:, :width].astype(jnp.bfloat16)
    v_ref[...] = total[:, width:].astype(jnp.bfloat16)


def per_device(queries, key_states, value_states, out_grad, doc_lengths):
    rows, width = queries.shape
    kv_width = 2 * key_states.shape[1]
    kv_heads = kv_width // (2 * HD)
    group = width // HD // kv_heads
    half_cols = group * rows // HALVES
    cols = group * rows
    near_keys = (NEAR + 1) * rows
    keys = (REACH + 1) * rows
    bf16, f32 = jnp.bfloat16, jnp.float32
    array = jax.ShapeDtypeStruct
    narrow = array((rows, kv_width), bf16)
    wide = array((rows, width), bf16)
    first = (lax.axis_index(("ctx", "rep")) * rows).astype(jnp.int32).reshape(1)
    own, q, g, low = call(
        load_kernel,
        "load",
        [narrow, wide, wide, array((HALVES, half_cols), jnp.int32)],
        [pl.BlockSpec(memory_space=pltpu.SMEM)] + [HBM] * 5,
        [first]
        + [
            pltpu.with_memory_space_constraint(a, pltpu.MemorySpace.HBM)
            for a in (doc_lengths.reshape(1, -1), key_states, value_states, queries, out_grad)
        ],
        0,
        [pltpu.VMEM((1, doc_lengths.shape[0]), jnp.int32), pltpu.SemaphoreType.DMA((5,))],
    )
    received = {distance: shifted(own, distance) for distance in (4, 3, 1, 2)}
    blocks = [received[distance] for distance in range(REACH, 0, -1)] + [own]
    work = 2 * HD * rows * cols * kv_heads
    p, d, stat = call(
        near_kernel,
        "near",
        [array((kv_heads, near_keys, cols), f32)] * 2 + [array((kv_heads, 2, cols), f32)],
        [VMEM] * (4 + NEAR),
        [low, q, g] + blocks[REACH - 1 : REACH - NEAR - 1 : -1] + [own],
        2 * (NEAR + 1) * work,
    )
    *terms, att, ds, own_p = call(
        terms_kernel,
        "terms",
        [narrow] * REACH
        + [
            array((kv_heads, HD, cols), bf16),
            array((kv_heads, keys, cols), bf16),
            array((kv_heads, rows, cols), bf16),
        ],
        [VMEM] * (7 + REACH),
        [low, q, g, p, d, stat] + blocks,
        (3 * REACH + 5) * work,
        [pltpu.VMEM((keys, cols), bf16)],
    )
    returned = {distance: shifted(terms[REACH - distance], -distance) for distance in (2, 1, 3, 4)}
    attended, query_grad, total = call(
        own_kernel,
        "own",
        [wide, wide, array((rows, kv_width), f32)],
        [VMEM] * (6 + REACH),
        [q, g, att, ds, own_p] + blocks,
        (REACH + 3) * work,
    )
    key_grad, value_grad = call(
        add_kernel,
        "add",
        [array(key_states.shape, bf16)] * 2,
        [VMEM] * (1 + REACH),
        [total] + list(returned.values()),
        0,
    )
    return attended, query_grad, key_grad, value_grad


def solution(mesh):
    split = P(("ctx", "rep"), "tp")
    return jax.shard_map(
        per_device,
        mesh=mesh,
        in_specs=(split, split, split, split, P()),
        out_specs=(split, split, split, split),
        check_vma=False,
    )
```

time: 55.2 us -> 47.1 us (0.85)
  the two profiles are of different devices: /device:TPU:643 before, /device:TPU:1 now
where the time goes in v2:
time: 47.1 us; the launch traced here: 46.8 us
  starting transfers between devices  30 us (64%)
  Pallas kernels  9.79 us (21%)
  waiting for transfers between devices  6.25 us (13%)
  between operations  0.74 us (2%)
    ppermute x8, starting transfers between devices, shifted(): return lax.ppermute(block, axes, route)  30 us
    pallas_call x5, Pallas kernels, call(): pl.pallas_call(kernel, out_shape=tuple(outs), in_specs=specs, out_specs=(...  9.79 us
    ppermute x8, waiting for transfers between devices, shifted(): return lax.ppermute(block, axes, route)  6.25 us
  transfers between devices with their start and end apart: 8, of which 3 were waited for; matrix products, arithmetic and copies ran while one was open for 0% of the time, Pallas kernels for 7%

profile of v2, /device:TPU:1, one launch (start us, length us, event | category | flops | bytes accessed | tf_op | source)
XLA Modules:
  0.0 46.8 jit_solution(4282943441443121718)
XLA Ops:
  0.6 1.3 %load.1 = (bf16[192,512]{1,0:T(8,128)(2,1)S(1)}, bf16[192,1024]{1,0:T(8,128)(2,1)S(1)}, bf16[192,1024]{1,0:T(8,128)(2,1)S(1)}, s32[2,384]{1,0:T(2,128)S(1)}) custom-call(s32[1]{0:T(128)} %bitcast.first_ref, s32[1,255]{1,0:T(1,128)} %bitcast.2, bf16[192,256]{1,0:T(8,128)(2,1)} %k_hbm.1, bf16[192,256]{1,0:T(8,128)(2,1)} %v_hbm.1, bf16[192,1024]{1,0:T(8,128)(2,1)} %q_hbm.1, ...), custom_call_target="tpu_custom_call" | custom-call | bytes 1970176 | tf_op jit(solution)/shard_map/load/pallas_call | solution.py:36
  1.9 5.5 %collective-permute-start.1 = (bf16[192,512]{1,0:T(8,128)(2,1)S(1)}, bf16[192,512]{1,0:T(8,128)(2,1)S(1)}, u32[]{:S(2)}, u32[]{:S(2)}) collective-permute-start(bf16[192,512]{1,0:T(8,128)(2,1)S(1)} %get-tuple-element.26.refs_2_.refs_4_), channel_id=1, source_target_pairs={{0,2},{1,3},{2,16},{3,17},{16,18},{17,19},{18,32},{19,33},{32,34},... | collective-permute-start | bytes 589832 | tf_op jit(solution)/shard_map/ppermute | solution.py:25
  7.4 2.2 %collective-permute-start = (bf16[192,512]{1,0:T(8,128)(2,1)S(1)}, bf16[192,512]{1,0:T(8,128)(2,1)S(1)}, u32[]{:S(2)}, u32[]{:S(2)}) collective-permute-start(bf16[192,512]{1,0:T(8,128)(2,1)S(1)} %get-tuple-element.26.refs_2_.refs_4_), channel_id=1, source_target_pairs={{0,1},{1,2},{2,3},{3,16},{16,17},{17,18},{18,19},{19,32},{32,33},{... | collective-permute-start | bytes 589832 | tf_op jit(solution)/shard_map/ppermute | solution.py:25
  9.6 6.1 %collective-permute-start.3 = (bf16[192,512]{1,0:T(8,128)(2,1)S(1)}, bf16[192,512]{1,0:T(8,128)(2,1)S(1)}, u32[]{:S(2)}, u32[]{:S(2)}) collective-permute-start(bf16[192,512]{1,0:T(8,128)(2,1)S(1)} %get-tuple-element.26.refs_2_.refs_4_), channel_id=1, source_target_pairs={{0,3},{1,16},{2,17},{3,18},{16,19},{17,32},{18,33},{19,34},{32,35}... | collective-permute-start | bytes 589832 | tf_op jit(solution)/shard_map/ppermute | solution.py:25
  15.8 1.9 %collective-permute-start.2 = (bf16[192,512]{1,0:T(8,128)(2,1)S(1)}, bf16[192,512]{1,0:T(8,128)(2,1)S(1)}, u32[]{:S(2)}, u32[]{:S(2)}) collective-permute-start(bf16[192,512]{1,0:T(8,128)(2,1)S(1)} %get-tuple-element.26.refs_2_.refs_4_), channel_id=1, source_target_pairs={{0,16},{1,17},{2,18},{3,19},{16,32},{17,33},{18,34},{19,35},{32,48... | collective-permute-start | bytes 589832 | tf_op jit(solution)/shard_map/ppermute | solution.py:25
  17.7 0.0 collective-permute-done.1.refs_1_.refs_2_
  17.7 0.0 collective-permute-done.refs_0_.refs_3_
  17.7 1.3 %near.1 = (f32[2,576,768]{2,1,0:T(8,128)S(1)}, f32[2,576,768]{2,1,0:T(8,128)S(1)}, f32[2,2,768]{2,1,0:T(2,128)S(1)}) custom-call(s32[2,384]{1,0:T(2,128)S(1)} %get-tuple-element.25.low_ref, bf16[192,1024]{1,0:T(8,128)(2,1)S(1)} %get-tuple-element.23.q_ref, bf16[192,1024]{1,0:T(8,128)(2,1)S(1)} %get-tuple-element.24.g_ref, ...), custom_call_target="tpu_custom_call" | custom-call | flops 452984832 | bytes 8469504 | tf_op jit(solution)/shard_map/near/pallas_call | solution.py:36
  19.1 0.0 collective-permute-done.3.refs_1_
  19.1 3.1 %collective-permute-done.2.refs_0_ = bf16[192,512]{1,0:T(8,128)(2,1)S(1)} collective-permute-done((bf16[192,512]{1,0:T(8,128)(2,1)S(1)}, bf16[192,512]{1,0:T(8,128)(2,1)S(1)}, u32[]{:S(2)}, u32[]{:S(2)}) %collective-permute-start.2) | collective-permute-done | bytes 196640 | tf_op jit(solution)/shard_map/ppermute | solution.py:25
  22.2 4.5 %terms.1 = (bf16[192,512]{1,0:T(8,128)(2,1)S(1)}, bf16[192,512]{1,0:T(8,128)(2,1)S(1)}, bf16[192,512]{1,0:T(8,128)(2,1)S(1)}, bf16[192,512]{1,0:T(8,128)(2,1)S(1...) custom-call(s32[2,384]{1,0:T(2,128)S(1)} %get-tuple-element.25.low_ref, ...), custom_call_target="tpu_custom_call" | custom-call | flops 1283457024 | bytes 13581312 | tf_op jit(solution)/shard_map/terms/pallas_call | solution.py:36
  26.7 5.2 %collective-permute-start.4 = (bf16[192,512]{1,0:T(8,128)(2,1)S(1)}, bf16[192,512]{1,0:T(8,128)(2,1)S(1)}, u32[]{:S(2)}, u32[]{:S(2)}) collective-permute-start(bf16[192,512]{1,0:T(8,128)(2,1)S(1)} %get-tuple-element.36), channel_id=1, source_target_pairs={{2,0},{3,1},{16,2},{17,3},{18,16},{19,17},{32,18},{33,19},{34,32},... | collective-permute-start | bytes 589832 | tf_op jit(solution)/shard_map/ppermute | solution.py:25
  31.9 5.2 %collective-permute-start.5 = (bf16[192,512]{1,0:T(8,128)(2,1)S(1)}, bf16[192,512]{1,0:T(8,128)(2,1)S(1)}, u32[]{:S(2)}, u32[]{:S(2)}) collective-permute-start(bf16[192,512]{1,0:T(8,128)(2,1)S(1)} %get-tuple-element.37), channel_id=1, source_target_pairs={{1,0},{2,1},{3,2},{16,3},{17,16},{18,17},{19,18},{32,19},{33,32},{... | collective-permute-start | bytes 589832 | tf_op jit(solution)/shard_map/ppermute | solution.py:25
  37.1 1.9 %collective-permute-start.6 = (bf16[192,512]{1,0:T(8,128)(2,1)S(1)}, bf16[192,512]{1,0:T(8,128)(2,1)S(1)}, u32[]{:S(2)}, u32[]{:S(2)}) collective-permute-start(bf16[192,512]{1,0:T(8,128)(2,1)S(1)} %get-tuple-element.38), channel_id=1, source_target_pairs={{3,0},{16,1},{17,2},{18,3},{19,16},{32,17},{33,18},{34,19},{35,32}... | collective-permute-start | bytes 589832 | tf_op jit(solution)/shard_map/ppermute | solution.py:25
  39.0 1.9 %collective-permute-start.7 = (bf16[192,512]{1,0:T(8,128)(2,1)S(1)}, bf16[192,512]{1,0:T(8,128)(2,1)S(1)}, u32[]{:S(2)}, u32[]{:S(2)}) collective-permute-start(bf16[192,512]{1,0:T(8,128)(2,1)S(1)} %get-tuple-element.39), channel_id=1, source_target_pairs={{16,0},{17,1},{18,2},{19,3},{32,16},{33,17},{34,18},{35,19},{48,32... | collective-permute-start | bytes 589832 | tf_op jit(solution)/shard_map/ppermute | solution.py:25
  41.0 1.9 %own.1 = (bf16[192,1024]{1,0:T(8,128)(2,1)}, bf16[192,1024]{1,0:T(8,128)(2,1)}, f32[192,512]{1,0:T(8,128)S(1)}) custom-call(bf16[192,1024]{1,0:T(8,128)(2,1)S(1)} %get-tuple-element.23.q_ref, bf16[192,1024]{1,0:T(8,128)(2,1)S(1)} %get-tuple-element.24.g_ref, bf16[2,128,768]{2,1,0:T(8,128)(2,1)S(1)} %get-tuple-element.30.att_ref, ...), custom_call_target="tpu_custom_call" | custom-call | flops 528482304 | bytes 6881280 | tf_op jit(solution)/shard_map/own/pallas_call | solution.py:36
  42.9 0.0 collective-permute-done.4.refs_0_
  42.9 0.0 collective-permute-done.5.refs_1_
  42.9 1.8 %collective-permute-done.6.refs_2_ = bf16[192,512]{1,0:T(8,128)(2,1)S(1)} collective-permute-done((bf16[192,512]{1,0:T(8,128)(2,1)S(1)}, bf16[192,512]{1,0:T(8,128)(2,1)S(1)}, u32[]{:S(2)}, u32[]{:S(2)}) %collective-permute-start.6) | collective-permute-done | bytes 196640 | tf_op jit(solution)/shard_map/ppermute | solution.py:25
  44.7 1.3 %collective-permute-done.7.refs_3_ = bf16[192,512]{1,0:T(8,128)(2,1)S(1)} collective-permute-done((bf16[192,512]{1,0:T(8,128)(2,1)S(1)}, bf16[192,512]{1,0:T(8,128)(2,1)S(1)}, u32[]{:S(2)}, u32[]{:S(2)}) %collective-permute-start.7) | collective-permute-done | bytes 196640 | tf_op jit(solution)/shard_map/ppermute | solution.py:25
  46.0 0.8 %add.5 = (bf16[192,256]{1,0:T(8,128)(2,1)}, bf16[192,256]{1,0:T(8,128)(2,1)}) custom-call(f32[192,512]{1,0:T(8,128)S(1)} %get-tuple-element.35.total_ref, bf16[192,512]{1,0:T(8,128)(2,1)S(1)} %collective-permute-done.4.refs_0_, bf16[192,512]{1,0:T(8,128)(2,1)S(1)} %collective-permute-done.5.refs_1_, bf16[192,512]{1,0:T(8,128)(2,1)S(1)} %collective-permute-done.6.refs_2_, ...), custom_call_target="tpu_custom_call" | custom-call | bytes 1376256 | tf_op jit(solution)/shard_map/add/pallas_call | solution.py:36
Async XLA Ops:
  1.9 15.8 %collective-permute-start.1 = (bf16[192,512]{1,0:T(8,128)(2,1)S(1)}, bf16[192,512]{1,0:T(8,128)(2,1)S(1)}, u32[]{:S(2)}, u32[]{:S(2)}) collective-permute-start(bf16[192,512]{1,0:T(8,128)(2,1)S(1)} %get-tuple-element.26.refs_2_.refs_4_), channel_id=1, source_target_pairs={{0,2},{1,3},{2,16},{3,17},{16,18},{17,19},{18,32},{19,33},{32,34},... | collective-permute-start | bytes 589832 | tf_op jit(solution)/shard_map/ppermute | solution.py:25
  7.4 10.3 %collective-permute-start = (bf16[192,512]{1,0:T(8,128)(2,1)S(1)}, bf16[192,512]{1,0:T(8,128)(2,1)S(1)}, u32[]{:S(2)}, u32[]{:S(2)}) collective-permute-start(bf16[192,512]{1,0:T(8,128)(2,1)S(1)} %get-tuple-element.26.refs_2_.refs_4_), channel_id=1, source_target_pairs={{0,1},{1,2},{2,3},{3,16},{16,17},{17,18},{18,19},{19,32},{32,33},{... | collective-permute-start | bytes 589832 | tf_op jit(solution)/shard_map/ppermute | solution.py:25
  9.6 9.4 %collective-permute-start.3 = (bf16[192,512]{1,0:T(8,128)(2,1)S(1)}, bf16[192,512]{1,0:T(8,128)(2,1)S(1)}, u32[]{:S(2)}, u32[]{:S(2)}) collective-permute-start(bf16[192,512]{1,0:T(8,128)(2,1)S(1)} %get-tuple-element.26.refs_2_.refs_4_), channel_id=1, source_target_pairs={{0,3},{1,16},{2,17},{3,18},{16,19},{17,32},{18,33},{19,34},{32,35}... | collective-permute-start | bytes 589832 | tf_op jit(solution)/shard_map/ppermute | solution.py:25
  15.8 6.4 %collective-permute-start.2 = (bf16[192,512]{1,0:T(8,128)(2,1)S(1)}, bf16[192,512]{1,0:T(8,128)(2,1)S(1)}, u32[]{:S(2)}, u32[]{:S(2)}) collective-permute-start(bf16[192,512]{1,0:T(8,128)(2,1)S(1)} %get-tuple-element.26.refs_2_.refs_4_), channel_id=1, source_target_pairs={{0,16},{1,17},{2,18},{3,19},{16,32},{17,33},{18,34},{19,35},{32,48... | collective-permute-start | bytes 589832 | tf_op jit(solution)/shard_map/ppermute | solution.py:25
  26.7 16.2 %collective-permute-start.4 = (bf16[192,512]{1,0:T(8,128)(2,1)S(1)}, bf16[192,512]{1,0:T(8,128)(2,1)S(1)}, u32[]{:S(2)}, u32[]{:S(2)}) collective-permute-start(bf16[192,512]{1,0:T(8,128)(2,1)S(1)} %get-tuple-element.36), channel_id=1, source_target_pairs={{2,0},{3,1},{16,2},{17,3},{18,16},{19,17},{32,18},{33,19},{34,32},... | collective-permute-start | bytes 589832 | tf_op jit(solution)/shard_map/ppermute | solution.py:25
  31.9 11.0 %collective-permute-start.5 = (bf16[192,512]{1,0:T(8,128)(2,1)S(1)}, bf16[192,512]{1,0:T(8,128)(2,1)S(1)}, u32[]{:S(2)}, u32[]{:S(2)}) collective-permute-start(bf16[192,512]{1,0:T(8,128)(2,1)S(1)} %get-tuple-element.37), channel_id=1, source_target_pairs={{1,0},{2,1},{3,2},{16,3},{17,16},{18,17},{19,18},{32,19},{33,32},{... | collective-permute-start | bytes 589832 | tf_op jit(solution)/shard_map/ppermute | solution.py:25
  37.1 7.6 %collective-permute-start.6 = (bf16[192,512]{1,0:T(8,128)(2,1)S(1)}, bf16[192,512]{1,0:T(8,128)(2,1)S(1)}, u32[]{:S(2)}, u32[]{:S(2)}) collective-permute-start(bf16[192,512]{1,0:T(8,128)(2,1)S(1)} %get-tuple-element.38), channel_id=1, source_target_pairs={{3,0},{16,1},{17,2},{18,3},{19,16},{32,17},{33,18},{34,19},{35,32}... | collective-permute-start | bytes 589832 | tf_op jit(solution)/shard_map/ppermute | solution.py:25
  39.0 7.0 %collective-permute-start.7 = (bf16[192,512]{1,0:T(8,128)(2,1)S(1)}, bf16[192,512]{1,0:T(8,128)(2,1)S(1)}, u32[]{:S(2)}, u32[]{:S(2)}) collective-permute-start(bf16[192,512]{1,0:T(8,128)(2,1)S(1)} %get-tuple-element.39), channel_id=1, source_target_pairs={{16,0},{17,1},{18,2},{19,3},{32,16},{33,17},{34,18},{35,19},{48,32... | collective-permute-start | bytes 589832 | tf_op jit(solution)/shard_map/ppermute | solution.py:25

commit v3 on v2

v3 whole, which is shorter than its diff:
```python
import math

import jax
import jax.numpy as jnp
from jax import lax
from jax.experimental import pallas as pl
from jax.experimental.pallas import tpu as pltpu
from jax.sharding import PartitionSpec as P

HD = 128
REACH = 4
ORDER = (4, 3, 1, 2, 0)
FAR = 3
HALVES = 2
MASKED = -1e30
SCALING = 1.0 / math.sqrt(HD)
EXP2_SCALING = SCALING * math.log2(math.e)
VMEM = pl.BlockSpec(memory_space=pltpu.VMEM)
HBM = pl.BlockSpec(memory_space=pltpu.MemorySpace.HBM)


def shifted(block, distance):
    axes = ("ctx", "rep")
    devices = range(lax.axis_size(axes))
    route = [(i, i + distance) for i in devices if i + distance in devices]
    return lax.ppermute(block, axes, route)


def contract(a, b, dim_a, dim_b):
    return lax.dot_general(
        a, b, (((dim_a,), (dim_b,)), ((), ())), preferred_element_type=jnp.float32
    )


def call(kernel, name, outs, specs, operands, flops, scratch=()):
    size = lambda a: math.prod(a.shape) * jnp.dtype(a.dtype).itemsize
    return pl.pallas_call(
        kernel,
        out_shape=tuple(outs),
        in_specs=specs,
        out_specs=(VMEM,) * len(outs),
        scratch_shapes=list(scratch),
        compiler_params=pltpu.CompilerParams(vmem_limit_bytes=24 << 20),
        cost_estimate=pl.CostEstimate(
            flops=flops,
            bytes_accessed=sum(map(size, (*operands, *outs))),
            transcendentals=0,
        ),
        name=name,
    )(*operands)


def window(distance):
    return ORDER.index(distance)


def key_cols(kv):
    return slice(kv * HD, (kv + 1) * HD)


def value_cols(kv, kv_heads):
    return slice((kv_heads + kv) * HD, (kv_heads + kv + 1) * HD)


def join_kernel(k_hbm, v_hbm, kv_ref, sems):
    width = k_hbm.shape[1]
    copies = [
        pltpu.make_async_copy(k_hbm, kv_ref.at[:, :width], sems.at[0]),
        pltpu.make_async_copy(v_hbm, kv_ref.at[:, width:], sems.at[1]),
    ]
    for copy in copies:
        copy.start()
    for copy in copies:
        copy.wait()


def load_kernel(
    first_ref, lengths_hbm, q_hbm, g_hbm, q_ref, g_ref, qt_ref, gt_ref, low_ref, *scratch
):
    lengths_ref, q_scr, g_scr, sems = scratch
    copies = [
        pltpu.make_async_copy(lengths_hbm, lengths_ref, sems.at[0]),
        pltpu.make_async_copy(q_hbm, q_scr, sems.at[1]),
        pltpu.make_async_copy(g_hbm, g_scr, sems.at[2]),
    ]
    for copy in copies:
        copy.start()
    copies[0].wait()
    rows = q_scr.shape[0]
    kv_heads, cols = q_ref.shape[:2]
    group = cols // rows
    part = rows // HALVES
    lengths = lengths_ref[...]
    docs = lengths.shape[1]
    upto = lax.broadcasted_iota(jnp.int32, (docs, docs), 1) <= lax.broadcasted_iota(
        jnp.int32, (docs, docs), 0
    )
    ends = jnp.sum(jnp.where(upto, lengths, 0), axis=1, keepdims=True)
    first = first_ref[0]
    pos = first + lax.broadcasted_iota(jnp.int32, (docs, rows), 1)
    begins = jnp.max(jnp.where(ends <= pos, ends, 0), axis=0, keepdims=True)
    low = begins - first + REACH * rows
    for half in range(HALVES):
        low_ref[half : half + 1] = jnp.concatenate(
            [low[:, half * part : (half + 1) * part]] * group, axis=1
        )
    for copy, scr, ref, t_ref in (
        (copies[1], q_scr, q_ref, qt_ref),
        (copies[2], g_scr, g_ref, gt_ref),
    ):
        copy.wait()
        for kv in range(kv_heads):
            tall = jnp.concatenate(
                [
                    scr[half * part : (half + 1) * part, h * HD : (h + 1) * HD]
                    for half in range(HALVES)
                    for h in range(kv * group, (kv + 1) * group)
                ],
                axis=0,
            )
            ref[kv] = tall
            t_ref[kv] = tall.T


def own_rows(rows, half):
    return (half + 1) * (rows // HALVES)


def keys_of(distances, rows, cols, skip=0):
    places = [
        lax.broadcasted_iota(jnp.int32, (rows, cols), 0) + (REACH - distance) * rows
        for distance in distances
    ]
    return jnp.concatenate(places, axis=0)[skip:]


def near_kernel(low_ref, qt_ref, gt_ref, *refs):
    kv_refs, (p_ref, d_ref, stat_ref) = refs[:-3], refs[-3:]
    rows = kv_refs[0].shape[0]
    kv_heads, _, all_cols = qt_ref.shape
    cols = all_cols // HALVES
    part = rows // HALVES
    before = (len(kv_refs) - 1) * rows
    for kv in range(kv_heads):
        for half in range(HALVES):
            own = own_rows(rows, half)
            keys = before + own
            tile = slice(half * cols, (half + 1) * cols)
            k = jnp.concatenate([r[:, key_cols(kv)] for r in kv_refs], axis=0)[:keys]
            v = jnp.concatenate([r[:, value_cols(kv, kv_heads)] for r in kv_refs], axis=0)[:keys]
            low = low_ref[half : half + 1]
            query = half * part + lax.broadcasted_iota(jnp.int32, (1, cols), 1) % part
            own_key = lax.broadcasted_iota(jnp.int32, (own, cols), 0)
            allowed = jnp.concatenate(
                [
                    keys_of(ORDER[FAR:-1], rows, cols) >= low,
                    (own_key + REACH * rows >= low) & (own_key <= query),
                ],
                axis=0,
            )
            s = jnp.where(allowed, contract(k, qt_ref[kv, :, tile], 1, 0), MASKED)
            top = jnp.max(s, axis=0, keepdims=True)
            p = jnp.exp2((s - top) * EXP2_SCALING)
            p_ref[kv, :keys, tile] = p
            d_ref[kv, :keys, tile] = contract(v, gt_ref[kv, :, tile], 1, 0)
            stat_ref[kv, 0:1, tile] = top
            stat_ref[kv, 1:2, tile] = jnp.sum(p, axis=0, keepdims=True)


def terms_kernel(low_ref, q_ref, g_ref, qt_ref, gt_ref, p_near_ref, d_near_ref, stat_ref, *refs):
    blocks = REACH + 1
    kv_refs, refs = refs[:blocks], refs[blocks:]
    term_refs, (att_ref, p_ref, ds_ref, p_scr, d_scr) = refs[:REACH], refs[REACH:]
    rows = kv_refs[0].shape[0]
    kv_heads, _, all_cols = qt_ref.shape
    cols = all_cols // HALVES
    part = rows // HALVES
    split = FAR * rows

    def kept(n, half):
        start = half * part if n == 0 else 0
        stop = own_rows(rows, half) if n == REACH else rows
        return slice(n * rows + start, n * rows + stop)

    def probs(kv, n, half):
        tile = slice(half * cols, (half + 1) * cols)
        here = kept(n, half)
        if n < FAR:
            return p_scr[kv, here, tile], d_scr[kv, here, tile]
        near = slice(here.start - split, here.stop - split)
        return p_near_ref[kv, near, tile], d_near_ref[kv, near, tile]

    def scores(kv, half):
        start = half * part
        tile = slice(half * cols, (half + 1) * cols)
        k = jnp.concatenate([r[:, key_cols(kv)] for r in kv_refs[:FAR]], axis=0)[start:]
        v = jnp.concatenate([r[:, value_cols(kv, kv_heads)] for r in kv_refs[:FAR]], axis=0)[start:]
        allowed = keys_of(ORDER[:FAR], rows, cols, start) >= low_ref[half : half + 1]
        s = jnp.where(allowed, contract(k, qt_ref[kv, :, tile], 1, 0), MASKED)
        near_top = stat_ref[kv, 0:1, tile]
        top = jnp.maximum(near_top, jnp.max(s, axis=0, keepdims=True))
        p = jnp.exp2((s - top) * EXP2_SCALING)
        p_scr[kv, start:split, tile] = p
        d_scr[kv, start:split, tile] = contract(v, gt_ref[kv, :, tile], 1, 0)
        ratio = jnp.exp2((near_top - top) * EXP2_SCALING)
        total = ratio * stat_ref[kv, 1:2, tile] + jnp.sum(p, axis=0, keepdims=True)
        inverse = 1.0 / total
        return inverse, ratio * inverse

    def attend(kv, half, scales):
        tile = slice(half * cols, (half + 1) * cols)
        att = jnp.zeros((HD, cols), jnp.float32)
        for n in range(blocks):
            here = kept(n, half)
            v = kv_refs[n][here.start - n * rows : here.stop - n * rows, value_cols(kv, kv_heads)]
            p_bf = (probs(kv, n, half)[0] * scales[n >= FAR]).astype(jnp.bfloat16)
            p_ref[kv, here, tile] = p_bf
            att = att + contract(v, p_bf, 0, 0)
        att = att.astype(jnp.bfloat16)
        att_ref[kv, :, tile] = att
        gt = gt_ref[kv, :, tile].astype(jnp.float32)
        return jnp.sum(gt * att.astype(jnp.float32), axis=0, keepdims=True)

    def send(kv, n, scales, deltas):
        for half in range(HALVES):
            tile = slice(half * cols, (half + 1) * cols)
            p, d = probs(kv, n, half)
            ds = (p * scales[half][n >= FAR]) * (d - deltas[half])
            ds_ref[kv, kept(n, half), tile] = ds.astype(jnp.bfloat16)
        if n < REACH:
            block = slice(n * rows, (n + 1) * rows)
            kg = contract(ds_ref[kv, block], q_ref[kv], 1, 0) * SCALING
            vg = contract(p_ref[kv, block], g_ref[kv], 1, 0)
            term_refs[n][:, key_cols(kv)] = kg.astype(jnp.bfloat16)
            term_refs[n][:, value_cols(kv, kv_heads)] = vg.astype(jnp.bfloat16)

    empty = jnp.zeros((part, cols), jnp.bfloat16)
    for kv in range(kv_heads):
        for ref in (p_ref, ds_ref):
            ref[kv, :part, cols:] = empty
            ref[kv, (blocks * rows - part) :, :cols] = empty
    scales = [[scores(kv, half) for half in range(HALVES)] for kv in range(kv_heads)]
    deltas = [[attend(kv, half, scales[kv][half]) for half in range(HALVES)] for kv in range(kv_heads)]
    for kv in range(kv_heads):
        for n in range(blocks):
            send(kv, n, scales[kv], deltas[kv])


def own_kernel(q_ref, g_ref, att_ref, p_ref, ds_ref, *refs):
    kv_refs, (att_out, qg_out, total_ref) = refs[:-3], refs[-3:]
    rows = kv_refs[0].shape[0]
    kv_heads, all_cols = q_ref.shape[:2]
    group = all_cols // rows
    cols = all_cols // HALVES
    part = rows // HALVES
    remote = REACH * rows
    for kv in range(kv_heads):
        k = jnp.concatenate([r[:, key_cols(kv)] for r in kv_refs], axis=0)
        total_ref[:, key_cols(kv)] = contract(ds_ref[kv, remote:], q_ref[kv], 1, 0) * SCALING
        total_ref[:, value_cols(kv, kv_heads)] = contract(p_ref[kv, remote:], g_ref[kv], 1, 0)
        for half in range(HALVES):
            tile = slice(half * cols, (half + 1) * cols)
            start = half * part
            stop = remote + own_rows(rows, half)
            qg = contract(k[start:stop], ds_ref[kv, start:stop, tile], 0, 0) * SCALING
            qg = qg.astype(jnp.bfloat16).T
            att = att_ref[kv, :, tile].T
            for n in range(group):
                h = kv * group + n
                out = (slice(start, start + part), slice(h * HD, (h + 1) * HD))
                att_out[out] = att[n * part : (n + 1) * part]
                qg_out[out] = qg[n * part : (n + 1) * part]


def add_kernel(total_ref, *refs):
    term_refs, (k_ref, v_ref) = refs[:REACH], refs[REACH:]
    width = k_ref.shape[1]
    total = total_ref[...]
    for term_ref in term_refs:
        total = total + term_ref[...].astype(jnp.float32)
    k_ref[...] = total[:, :width].astype(jnp.bfloat16)
    v_ref[...] = total[:, width:].astype(jnp.bfloat16)


def per_device(queries, key_states, value_states, out_grad, doc_lengths):
    rows, width = queries.shape
    kv_width = 2 * key_states.shape[1]
    kv_heads = kv_width // (2 * HD)
    cols = rows * (width // HD // kv_heads)
    near_keys = (REACH + 1 - FAR) * rows
    keys = (REACH + 1) * rows
    bf16, f32 = jnp.bfloat16, jnp.float32
    array = jax.ShapeDtypeStruct
    narrow = array((rows, kv_width), bf16)
    wide = array((rows, width), bf16)
    tall = array((kv_heads, cols, HD), bf16)
    turned = array((kv_heads, HD, cols), bf16)
    scores = array((kv_heads, keys, cols), bf16)
    near_scores = array((kv_heads, near_keys, cols), f32)
    dma = pltpu.SemaphoreType.DMA
    work = 2 * HD * rows * cols * kv_heads
    first = (lax.axis_index(("ctx", "rep")) * rows).astype(jnp.int32).reshape(1)
    in_hbm = lambda a: pltpu.with_memory_space_constraint(a, pltpu.MemorySpace.HBM)

    (own,) = call(
        join_kernel,
        "join",
        [narrow],
        [HBM] * 2,
        [in_hbm(key_states), in_hbm(value_states)],
        0,
        [dma((2,))],
    )
    received = {distance: shifted(own, distance) for distance in (4, 3, 1, 2)}
    q, g, qt, gt, low = call(
        load_kernel,
        "load",
        [tall, tall, turned, turned, array((HALVES, cols // HALVES), jnp.int32)],
        [pl.BlockSpec(memory_space=pltpu.SMEM)] + [HBM] * 3,
        [first, in_hbm(doc_lengths.reshape(1, -1)), in_hbm(queries), in_hbm(out_grad)],
        0,
        [
            pltpu.VMEM((1, doc_lengths.shape[0]), jnp.int32),
            pltpu.VMEM(queries.shape, bf16),
            pltpu.VMEM(out_grad.shape, bf16),
            dma((3,)),
        ],
    )
    blocks = [received[distance] if distance else own for distance in ORDER]
    p, d, stat = call(
        near_kernel,
        "near",
        [near_scores, near_scores, array((kv_heads, 2, cols), f32)],
        [VMEM] * (4 + REACH - FAR),
        [low, qt, gt] + blocks[FAR:],
        2 * (REACH + 1 - FAR) * work,
    )
    *terms, att, p, ds = call(
        terms_kernel,
        "terms",
        [narrow] * REACH + [turned, scores, scores],
        [VMEM] * (9 + REACH),
        [low, q, g, qt, gt, p, d, stat] + blocks,
        (2 * FAR + 3 * REACH + 1) * work,
        [pltpu.VMEM((kv_heads, FAR * rows, cols), f32)] * 2,
    )
    returned = [shifted(terms[window(distance)], -distance) for distance in (2, 1, 3, 4)]
    attended, query_grad, total = call(
        own_kernel,
        "own",
        [wide, wide, array((rows, kv_width), f32)],
        [VMEM] * (6 + REACH),
        [q, g, att, p, ds] + blocks,
        (REACH + 3) * work,
    )
    key_grad, value_grad = call(
        add_kernel,
        "add",
        [array(key_states.shape, bf16)] * 2,
        [VMEM] * (1 + REACH),
        [total] + returned,
        0,
    )
    return attended, query_grad, key_grad, value_grad


def solution(mesh):
    split = P(("ctx", "rep"), "tp")
    return jax.shard_map(
        per_device,
        mesh=mesh,
        in_specs=(split, split, split, split, P()),
        out_specs=(split, split, split, split),
        check_vma=False,
    )
```

time: 47.1 us -> 45.7 us (0.970)
  starting transfers between devices: 30 us -> 28.6 us
  waiting for transfers between devices: 6.25 us -> 5.28 us
  Pallas kernels: 9.79 us -> 10.4 us
    ppermute x8, starting transfers between devices: 30 us -> 28.6 us  [shifted(): return lax.ppermute(block, axes, route)]
    ppermute x8, waiting for transfers between devices: 6.25 us -> 5.28 us  [shifted(): return lax.ppermute(block, axes, route)]
    pallas_call x5 -> x6, Pallas kernels: 9.79 us -> 10.4 us  [call(): pl.pallas_call(kernel, out_shape=tuple(outs), in_specs=specs, out_specs=(...]
  transfers between devices with their start and end apart: 8 -> 8, of which waited for: 3 -> 4; matrix products, arithmetic and copies ran while one was open for 0% -> 0% of each run, Pallas kernels for 7% -> 9%
where the time goes in v3:
time: 45.7 us; the launch traced here: 45.1 us
  starting transfers between devices  28.6 us (63%)
  Pallas kernels  10.4 us (23%)
  waiting for transfers between devices  5.28 us (12%)
  between operations  0.75 us (2%)
    ppermute x8, starting transfers between devices, shifted(): return lax.ppermute(block, axes, route)  28.6 us
    pallas_call x6, Pallas kernels, call(): pl.pallas_call(kernel, out_shape=tuple(outs), in_specs=specs, out_specs=(...  10.4 us
    ppermute x8, waiting for transfers between devices, shifted(): return lax.ppermute(block, axes, route)  5.28 us
  transfers between devices with their start and end apart: 8, of which 4 were waited for; matrix products, arithmetic and copies ran while one was open for 0% of the time, Pallas kernels for 9%

profile of v3, /device:TPU:1, one launch (start us, length us, event | category | flops | bytes accessed | tf_op | source)
XLA Modules:
  0.0 45.1 jit_solution(2684033335705586985)
XLA Ops:
  0.6 1.0 %join.1.refs_1_.refs_4_ = bf16[192,512]{1,0:T(8,128)(2,1)S(1)} custom-call(bf16[192,256]{1,0:T(8,128)(2,1)} %k_hbm.1, bf16[192,256]{1,0:T(8,128)(2,1)} %v_hbm.1), custom_call_target="tpu_custom_call" | custom-call | bytes 393216 | tf_op jit(solution)/shard_map/join/pallas_call | solution.py:37
  1.6 5.5 %collective-permute-start = (bf16[192,512]{1,0:T(8,128)(2,1)S(1)}, bf16[192,512]{1,0:T(8,128)(2,1)S(1)}, u32[]{:S(2)}, u32[]{:S(2)}) collective-permute-start(bf16[192,512]{1,0:T(8,128)(2,1)S(1)} %join.1.refs_1_.refs_4_), channel_id=1, source_target_pairs={{0,2},{1,3},{2,16},{3,17},{16,18},{17,19},{18,32},{19,33},{32,34},... | collective-permute-start | bytes 589832 | tf_op jit(solution)/shard_map/ppermute | solution.py:26
  7.1 2.2 %collective-permute-start.3 = (bf16[192,512]{1,0:T(8,128)(2,1)S(1)}, bf16[192,512]{1,0:T(8,128)(2,1)S(1)}, u32[]{:S(2)}, u32[]{:S(2)}) collective-permute-start(bf16[192,512]{1,0:T(8,128)(2,1)S(1)} %join.1.refs_1_.refs_4_), channel_id=1, source_target_pairs={{0,1},{1,2},{2,3},{3,16},{16,17},{17,18},{18,19},{19,32},{32,33},{... | collective-permute-start | bytes 589832 | tf_op jit(solution)/shard_map/ppermute | solution.py:26
  9.3 6.1 %collective-permute-start.2 = (bf16[192,512]{1,0:T(8,128)(2,1)S(1)}, bf16[192,512]{1,0:T(8,128)(2,1)S(1)}, u32[]{:S(2)}, u32[]{:S(2)}) collective-permute-start(bf16[192,512]{1,0:T(8,128)(2,1)S(1)} %join.1.refs_1_.refs_4_), channel_id=1, source_target_pairs={{0,3},{1,16},{2,17},{3,18},{16,19},{17,32},{18,33},{19,34},{32,35}... | collective-permute-start | bytes 589832 | tf_op jit(solution)/shard_map/ppermute | solution.py:26
  15.4 1.9 %collective-permute-start.1 = (bf16[192,512]{1,0:T(8,128)(2,1)S(1)}, bf16[192,512]{1,0:T(8,128)(2,1)S(1)}, u32[]{:S(2)}, u32[]{:S(2)}) collective-permute-start(bf16[192,512]{1,0:T(8,128)(2,1)S(1)} %join.1.refs_1_.refs_4_), channel_id=1, source_target_pairs={{0,16},{1,17},{2,18},{3,19},{16,32},{17,33},{18,34},{19,35},{32,48... | collective-permute-start | bytes 589832 | tf_op jit(solution)/shard_map/ppermute | solution.py:26
  17.4 1.4 %load.1 = (bf16[2,768,128]{2,1,0:T(8,128)(2,1)S(1)}, bf16[2,768,128]{2,1,0:T(8,128)(2,1)S(1)}, bf16[2,128,768]{2,1,0:T(8,128)(2,1)S(1)}, bf16[2,128,768]{2,1,0:T(8,128)(2,1)S(1)}, s32[2,384]{1,0:T(2,128)S(1)}) custom-call(s32[1]{0:T(128)} %bitcast.first_ref, s32[1,255]{1,0:T(1,128)} %bitcast.2, bf16[192,1024]{1,0:T(8,128)(2,1)} %q_hbm.1, bf16[192,1024]{1,0:T(8,128)(2,1)} %g_hbm.1), custom_call_target="tpu_custom_call" | custom-call | bytes 2363392 | tf_op jit(solution)/shard_map/load/pallas_call | solution.py:37
  18.8 0.0 collective-permute-done.refs_0_.refs_3_
  18.8 0.9 %near.1 = (f32[2,384,768]{2,1,0:T(8,128)S(1)}, f32[2,384,768]{2,1,0:T(8,128)S(1)}, f32[2,2,768]{2,1,0:T(2,128)S(1)}) custom-call(s32[2,384]{1,0:T(2,128)S(1)} %get-tuple-element.26.low_ref, bf16[2,128,768]{2,1,0:T(8,128)(2,1)S(1)} %get-tuple-element.27.qt_ref, bf16[2,128,768]{2,1,0:T(8,128)(2,1)S(1)} %get-tuple-element.28.gt_ref, ...), custom_call_target="tpu_custom_call" | custom-call | flops 301989888 | bytes 5913600 | tf_op jit(solution)/shard_map/near/pallas_call | solution.py:37
  19.7 0.0 collective-permute-done.3.refs_2_
  19.7 0.0 collective-permute-done.2.refs_1_
  19.7 2.2 %collective-permute-done.1.refs_0_ = bf16[192,512]{1,0:T(8,128)(2,1)S(1)} collective-permute-done((bf16[192,512]{1,0:T(8,128)(2,1)S(1)}, bf16[192,512]{1,0:T(8,128)(2,1)S(1)}, u32[]{:S(2)}, u32[]{:S(2)}) %collective-permute-start.1) | collective-permute-done | bytes 196640 | tf_op jit(solution)/shard_map/ppermute | solution.py:26
  21.9 4.5 %terms.1 = (bf16[192,512]{1,0:T(8,128)(2,1)S(1)}, bf16[192,512]{1,0:T(8,128)(2,1)S(1)}, bf16[192,512]{1,0:T(8,128)(2,1)S(1)}, bf16[192,512]{1,0:T(8,128)(2,1)S(1...) custom-call(s32[2,384]{1,0:T(2,128)S(1)} %get-tuple-element.26.low_ref, ...), custom_call_target="tpu_custom_call" | custom-call | flops 1434451968 | bytes 14367744 | tf_op jit(solution)/shard_map/terms/pallas_call | solution.py:37
  26.4 4.7 %collective-permute-start.4 = (bf16[192,512]{1,0:T(8,128)(2,1)S(1)}, bf16[192,512]{1,0:T(8,128)(2,1)S(1)}, u32[]{:S(2)}, u32[]{:S(2)}) collective-permute-start(bf16[192,512]{1,0:T(8,128)(2,1)S(1)} %get-tuple-element.38), channel_id=1, source_target_pairs={{2,0},{3,1},{16,2},{17,3},{18,16},{19,17},{32,18},{33,19},{34,32},... | collective-permute-start | bytes 589832 | tf_op jit(solution)/shard_map/ppermute | solution.py:26
  31.1 4.3 %collective-permute-start.5 = (bf16[192,512]{1,0:T(8,128)(2,1)S(1)}, bf16[192,512]{1,0:T(8,128)(2,1)S(1)}, u32[]{:S(2)}, u32[]{:S(2)}) collective-permute-start(bf16[192,512]{1,0:T(8,128)(2,1)S(1)} %get-tuple-element.39), channel_id=1, source_target_pairs={{1,0},{2,1},{3,2},{16,3},{17,16},{18,17},{19,18},{32,19},{33,32},{... | collective-permute-start | bytes 589832 | tf_op jit(solution)/shard_map/ppermute | solution.py:26
  35.4 1.9 %collective-permute-start.6 = (bf16[192,512]{1,0:T(8,128)(2,1)S(1)}, bf16[192,512]{1,0:T(8,128)(2,1)S(1)}, u32[]{:S(2)}, u32[]{:S(2)}) collective-permute-start(bf16[192,512]{1,0:T(8,128)(2,1)S(1)} %get-tuple-element.40), channel_id=1, source_target_pairs={{3,0},{16,1},{17,2},{18,3},{19,16},{32,17},{33,18},{34,19},{35,32}... | collective-permute-start | bytes 589832 | tf_op jit(solution)/shard_map/ppermute | solution.py:26
  37.3 1.9 %collective-permute-start.7 = (bf16[192,512]{1,0:T(8,128)(2,1)S(1)}, bf16[192,512]{1,0:T(8,128)(2,1)S(1)}, u32[]{:S(2)}, u32[]{:S(2)}) collective-permute-start(bf16[192,512]{1,0:T(8,128)(2,1)S(1)} %get-tuple-element.41), channel_id=1, source_target_pairs={{16,0},{17,1},{18,2},{19,3},{32,16},{33,17},{34,18},{35,19},{48,32... | collective-permute-start | bytes 589832 | tf_op jit(solution)/shard_map/ppermute | solution.py:26
  39.2 1.9 %own.1 = (bf16[192,1024]{1,0:T(8,128)(2,1)}, bf16[192,1024]{1,0:T(8,128)(2,1)}, f32[192,512]{1,0:T(8,128)S(1)}) custom-call(bf16[2,768,128]{2,1,0:T(8,128)(2,1)S(1)} %get-tuple-element.24.q_ref, bf16[2,768,128]{2,1,0:T(8,128)(2,1)S(1)} %get-tuple-element.25.g_ref, bf16[2,128,768]{2,1,0:T(8,128)(2,1)S(1)} %get-tuple-element.32.att_ref, ...), custom_call_target="tpu_custom_call" | custom-call | flops 528482304 | bytes 9240576 | tf_op jit(solution)/shard_map/own/pallas_call | solution.py:37
  41.2 0.0 collective-permute-done.4.refs_0_
  41.2 1.2 %collective-permute-done.5.refs_1_ = bf16[192,512]{1,0:T(8,128)(2,1)S(1)} collective-permute-done((bf16[192,512]{1,0:T(8,128)(2,1)S(1)}, bf16[192,512]{1,0:T(8,128)(2,1)S(1)}, u32[]{:S(2)}, u32[]{:S(2)}) %collective-permute-start.5) | collective-permute-done | bytes 196640 | tf_op jit(solution)/shard_map/ppermute | solution.py:26
  42.4 0.6 %collective-permute-done.6.refs_2_ = bf16[192,512]{1,0:T(8,128)(2,1)S(1)} collective-permute-done((bf16[192,512]{1,0:T(8,128)(2,1)S(1)}, bf16[192,512]{1,0:T(8,128)(2,1)S(1)}, u32[]{:S(2)}, u32[]{:S(2)}) %collective-permute-start.6) | collective-permute-done | bytes 196640 | tf_op jit(solution)/shard_map/ppermute | solution.py:26
  43.0 1.3 %collective-permute-done.7.refs_3_ = bf16[192,512]{1,0:T(8,128)(2,1)S(1)} collective-permute-done((bf16[192,512]{1,0:T(8,128)(2,1)S(1)}, bf16[192,512]{1,0:T(8,128)(2,1)S(1)}, u32[]{:S(2)}, u32[]{:S(2)}) %collective-permute-start.7) | collective-permute-done | bytes 196640 | tf_op jit(solution)/shard_map/ppermute | solution.py:26
  44.3 0.8 %add.5 = (bf16[192,256]{1,0:T(8,128)(2,1)}, bf16[192,256]{1,0:T(8,128)(2,1)}) custom-call(f32[192,512]{1,0:T(8,128)S(1)} %get-tuple-element.37.total_ref, bf16[192,512]{1,0:T(8,128)(2,1)S(1)} %collective-permute-done.4.refs_0_, bf16[192,512]{1,0:T(8,128)(2,1)S(1)} %collective-permute-done.5.refs_1_, bf16[192,512]{1,0:T(8,128)(2,1)S(1)} %collective-permute-done.6.refs_2_, ...), custom_call_target="tpu_custom_call" | custom-call | bytes 1376256 | tf_op jit(solution)/shard_map/add/pallas_call | solution.py:37
Async XLA Ops:
  1.6 17.2 %collective-permute-start = (bf16[192,512]{1,0:T(8,128)(2,1)S(1)}, bf16[192,512]{1,0:T(8,128)(2,1)S(1)}, u32[]{:S(2)}, u32[]{:S(2)}) collective-permute-start(bf16[192,512]{1,0:T(8,128)(2,1)S(1)} %join.1.refs_1_.refs_4_), channel_id=1, source_target_pairs={{0,2},{1,3},{2,16},{3,17},{16,18},{17,19},{18,32},{19,33},{32,34},... | collective-permute-start | bytes 589832 | tf_op jit(solution)/shard_map/ppermute | solution.py:26
  7.1 12.6 %collective-permute-start.3 = (bf16[192,512]{1,0:T(8,128)(2,1)S(1)}, bf16[192,512]{1,0:T(8,128)(2,1)S(1)}, u32[]{:S(2)}, u32[]{:S(2)}) collective-permute-start(bf16[192,512]{1,0:T(8,128)(2,1)S(1)} %join.1.refs_1_.refs_4_), channel_id=1, source_target_pairs={{0,1},{1,2},{2,3},{3,16},{16,17},{17,18},{18,19},{19,32},{32,33},{... | collective-permute-start | bytes 589832 | tf_op jit(solution)/shard_map/ppermute | solution.py:26
  9.3 10.4 %collective-permute-start.2 = (bf16[192,512]{1,0:T(8,128)(2,1)S(1)}, bf16[192,512]{1,0:T(8,128)(2,1)S(1)}, u32[]{:S(2)}, u32[]{:S(2)}) collective-permute-start(bf16[192,512]{1,0:T(8,128)(2,1)S(1)} %join.1.refs_1_.refs_4_), channel_id=1, source_target_pairs={{0,3},{1,16},{2,17},{3,18},{16,19},{17,32},{18,33},{19,34},{32,35}... | collective-permute-start | bytes 589832 | tf_op jit(solution)/shard_map/ppermute | solution.py:26
  15.4 6.4 %collective-permute-start.1 = (bf16[192,512]{1,0:T(8,128)(2,1)S(1)}, bf16[192,512]{1,0:T(8,128)(2,1)S(1)}, u32[]{:S(2)}, u32[]{:S(2)}) collective-permute-start(bf16[192,512]{1,0:T(8,128)(2,1)S(1)} %join.1.refs_1_.refs_4_), channel_id=1, source_target_pairs={{0,16},{1,17},{2,18},{3,19},{16,32},{17,33},{18,34},{19,35},{32,48... | collective-permute-start | bytes 589832 | tf_op jit(solution)/shard_map/ppermute | solution.py:26
  26.4 14.8 %collective-permute-start.4 = (bf16[192,512]{1,0:T(8,128)(2,1)S(1)}, bf16[192,512]{1,0:T(8,128)(2,1)S(1)}, u32[]{:S(2)}, u32[]{:S(2)}) collective-permute-start(bf16[192,512]{1,0:T(8,128)(2,1)S(1)} %get-tuple-element.38), channel_id=1, source_target_pairs={{2,0},{3,1},{16,2},{17,3},{18,16},{19,17},{32,18},{33,19},{34,32},... | collective-permute-start | bytes 589832 | tf_op jit(solution)/shard_map/ppermute | solution.py:26
  31.1 11.3 %collective-permute-start.5 = (bf16[192,512]{1,0:T(8,128)(2,1)S(1)}, bf16[192,512]{1,0:T(8,128)(2,1)S(1)}, u32[]{:S(2)}, u32[]{:S(2)}) collective-permute-start(bf16[192,512]{1,0:T(8,128)(2,1)S(1)} %get-tuple-element.39), channel_id=1, source_target_pairs={{1,0},{2,1},{3,2},{16,3},{17,16},{18,17},{19,18},{32,19},{33,32},{... | collective-permute-start | bytes 589832 | tf_op jit(solution)/shard_map/ppermute | solution.py:26
  35.4 7.6 %collective-permute-start.6 = (bf16[192,512]{1,0:T(8,128)(2,1)S(1)}, bf16[192,512]{1,0:T(8,128)(2,1)S(1)}, u32[]{:S(2)}, u32[]{:S(2)}) collective-permute-start(bf16[192,512]{1,0:T(8,128)(2,1)S(1)} %get-tuple-element.40), channel_id=1, source_target_pairs={{3,0},{16,1},{17,2},{18,3},{19,16},{32,17},{33,18},{34,19},{35,32}... | collective-permute-start | bytes 589832 | tf_op jit(solution)/shard_map/ppermute | solution.py:26
  37.3 7.0 %collective-permute-start.7 = (bf16[192,512]{1,0:T(8,128)(2,1)S(1)}, bf16[192,512]{1,0:T(8,128)(2,1)S(1)}, u32[]{:S(2)}, u32[]{:S(2)}) collective-permute-start(bf16[192,512]{1,0:T(8,128)(2,1)S(1)} %get-tuple-element.41), channel_id=1, source_target_pairs={{16,0},{17,1},{18,2},{19,3},{32,16},{33,17},{34,18},{35,19},{48,32... | collective-permute-start | bytes 589832 | tf_op jit(solution)/shard_map/ppermute | solution.py:26

commit v4 on v3

--- a/solution.py
+++ b/solution.py
@@ -1,3 +1,4 @@
+import functools
 import math
 
 import jax
@@ -10,7 +11,7 @@
 HD = 128
 REACH = 4
 ORDER = (4, 3, 1, 2, 0)
-FAR = 3
+FAR, MID = 2, 1
 HALVES = 2
 MASKED = -1e30
 SCALING = 1.0 / math.sqrt(HD)
@@ -134,61 +135,70 @@
     return jnp.concatenate(places, axis=0)[skip:]
 
 
-def near_kernel(low_ref, qt_ref, gt_ref, *refs):
-    kv_refs, (p_ref, d_ref, stat_ref) = refs[:-3], refs[-3:]
+def partial_kernel(low_ref, qt_ref, gt_ref, *refs, distances):
+    before, kv_refs = refs[: len(refs) - 3 - len(distances)], refs[-3 - len(distances) : -3]
+    p_ref, d_ref, stat_ref = refs[-3:]
     rows = kv_refs[0].shape[0]
     kv_heads, _, all_cols = qt_ref.shape
     cols = all_cols // HALVES
     part = rows // HALVES
-    before = (len(kv_refs) - 1) * rows
     for kv in range(kv_heads):
         for half in range(HALVES):
+            low = low_ref[half : half + 1]
             own = own_rows(rows, half)
-            keys = before + own
-            tile = slice(half * cols, (half + 1) * cols)
-            k = jnp.concatenate([r[:, key_cols(kv)] for r in kv_refs], axis=0)[:keys]
-            v = jnp.concatenate([r[:, value_cols(kv, kv_heads)] for r in kv_refs], axis=0)[:keys]
-            low = low_ref[half : half + 1]
             query = half * part + lax.broadcasted_iota(jnp.int32, (1, cols), 1) % part
             own_key = lax.broadcasted_iota(jnp.int32, (own, cols), 0)
             allowed = jnp.concatenate(
                 [
-                    keys_of(ORDER[FAR:-1], rows, cols) >= low,
-                    (own_key + REACH * rows >= low) & (own_key <= query),
+                    keys_of([distance], rows, cols) >= low
+                    if distance
+                    else (own_key + REACH * rows >= low) & (own_key <= query)
+                    for distance in distances
                 ],
                 axis=0,
             )
+            keys = allowed.shape[0]
+            tile = slice(half * cols, (half + 1) * cols)
+            k = jnp.concatenate([r[:, key_cols(kv)] for r in kv_refs], axis=0)[:keys]
+            v = jnp.concatenate([r[:, value_cols(kv, kv_heads)] for r in kv_refs], axis=0)[:keys]
             s = jnp.where(allowed, contract(k, qt_ref[kv, :, tile], 1, 0), MASKED)
             top = jnp.max(s, axis=0, keepdims=True)
+            for ref in before:
+                top = jnp.maximum(top, ref[kv, 0:1, tile])
             p = jnp.exp2((s - top) * EXP2_SCALING)
+            total = jnp.sum(p, axis=0, keepdims=True)
+            for ref in before:
+                ratio = jnp.exp2((ref[kv, 0:1, tile] - top) * EXP2_SCALING)
+                total = total + ratio * ref[kv, 1:2, tile]
+                stat_ref[kv, 2:3, tile] = ratio
             p_ref[kv, :keys, tile] = p
             d_ref[kv, :keys, tile] = contract(v, gt_ref[kv, :, tile], 1, 0)
             stat_ref[kv, 0:1, tile] = top
-            stat_ref[kv, 1:2, tile] = jnp.sum(p, axis=0, keepdims=True)
-
-
-def terms_kernel(low_ref, q_ref, g_ref, qt_ref, gt_ref, p_near_ref, d_near_ref, stat_ref, *refs):
+            stat_ref[kv, 1:2, tile] = total
+
+
+def terms_kernel(low_ref, q_ref, g_ref, qt_ref, gt_ref, *refs):
     blocks = REACH + 1
+    (p_mid_ref, d_mid_ref, mid_ref, p_near_ref, d_near_ref), refs = refs[:5], refs[5:]
     kv_refs, refs = refs[:blocks], refs[blocks:]
-    term_refs, (att_ref, p_ref, ds_ref, p_scr, d_scr) = refs[:REACH], refs[REACH:]
+    term_refs, (att_ref, p_ref, ds_ref, row_ref, p_scr, d_scr) = refs[:REACH], refs[REACH:]
     rows = kv_refs[0].shape[0]
     kv_heads, _, all_cols = qt_ref.shape
     cols = all_cols // HALVES
     part = rows // HALVES
-    split = FAR * rows
-
-    def kept(n, half):
+    group_of = [0] * FAR + [1] * MID + [2] * (blocks - FAR - MID)
+    firsts = [0, FAR, FAR + MID]
+    sources = [(p_scr, d_scr), (p_mid_ref, d_mid_ref), (p_near_ref, d_near_ref)]
+
+    def kept(n, half, base=0):
         start = half * part if n == 0 else 0
         stop = own_rows(rows, half) if n == REACH else rows
-        return slice(n * rows + start, n * rows + stop)
-
-    def probs(kv, n, half):
+        return slice((n - base) * rows + start, (n - base) * rows + stop)
+
+    def held(kv, n, half, which):
+        group = group_of[n]
         tile = slice(half * cols, (half + 1) * cols)
-        here = kept(n, half)
-        if n < FAR:
-            return p_scr[kv, here, tile], d_scr[kv, here, tile]
-        near = slice(here.start - split, here.stop - split)
-        return p_near_ref[kv, near, tile], d_near_ref[kv, near, tile]
+        return sources[group][which][kv, kept(n, half, firsts[group]), tile]
 
     def scores(kv, half):
         start = half * part
@@ -197,72 +207,81 @@
         v = jnp.concatenate([r[:, value_cols(kv, kv_heads)] for r in kv_refs[:FAR]], axis=0)[start:]
         allowed = keys_of(ORDER[:FAR], rows, cols, start) >= low_ref[half : half + 1]
         s = jnp.where(allowed, contract(k, qt_ref[kv, :, tile], 1, 0), MASKED)
-        near_top = stat_ref[kv, 0:1, tile]
-        top = jnp.maximum(near_top, jnp.max(s, axis=0, keepdims=True))
+        mid_top, mid_sum = mid_ref[kv, 0:1, tile], mid_ref[kv, 1:2, tile]
+        top = jnp.maximum(mid_top, jnp.max(s, axis=0, keepdims=True))
         p = jnp.exp2((s - top) * EXP2_SCALING)
-        p_scr[kv, start:split, tile] = p
-        d_scr[kv, start:split, tile] = contract(v, gt_ref[kv, :, tile], 1, 0)
-        ratio = jnp.exp2((near_top - top) * EXP2_SCALING)
-        total = ratio * stat_ref[kv, 1:2, tile] + jnp.sum(p, axis=0, keepdims=True)
-        inverse = 1.0 / total
-        return inverse, ratio * inverse
+        p_scr[kv, start : FAR * rows, tile] = p
+        d_scr[kv, start : FAR * rows, tile] = contract(v, gt_ref[kv, :, tile], 1, 0)
+        mid = jnp.exp2((mid_top - top) * EXP2_SCALING)
+        inverse = 1.0 / (mid * mid_sum + jnp.sum(p, axis=0, keepdims=True))
+        mid = mid * inverse
+        near = mid * mid_ref[kv, 2:3, tile]
+        row_ref[kv, 0:1, tile] = near
+        return inverse, mid, near
 
     def attend(kv, half, scales):
         tile = slice(half * cols, (half + 1) * cols)
-        att = jnp.zeros((HD, cols), jnp.float32)
+        parts, v = [], []
         for n in range(blocks):
-            here = kept(n, half)
-            v = kv_refs[n][here.start - n * rows : here.stop - n * rows, value_cols(kv, kv_heads)]
-            p_bf = (probs(kv, n, half)[0] * scales[n >= FAR]).astype(jnp.bfloat16)
-            p_ref[kv, here, tile] = p_bf
-            att = att + contract(v, p_bf, 0, 0)
+            p_bf = (held(kv, n, half, 0) * scales[group_of[n]]).astype(jnp.bfloat16)
+            p_ref[kv, kept(n, half), tile] = p_bf
+            parts.append(p_bf)
+            v.append(kv_refs[n][kept(n, half, n), value_cols(kv, kv_heads)])
+        att = contract(jnp.concatenate(v, axis=0), jnp.concatenate(parts, axis=0), 0, 0)
         att = att.astype(jnp.bfloat16)
         att_ref[kv, :, tile] = att
         gt = gt_ref[kv, :, tile].astype(jnp.float32)
-        return jnp.sum(gt * att.astype(jnp.float32), axis=0, keepdims=True)
-
-    def send(kv, n, scales, deltas):
-        for half in range(HALVES):
-            tile = slice(half * cols, (half + 1) * cols)
-            p, d = probs(kv, n, half)
-            ds = (p * scales[half][n >= FAR]) * (d - deltas[half])
+        delta = jnp.sum(gt * att.astype(jnp.float32), axis=0, keepdims=True)
+        row_ref[kv, 1:2, tile] = delta
+        return delta
+
+    def score_grads(kv, half, scales, delta):
+        tile = slice(half * cols, (half + 1) * cols)
+        for n in range(REACH):
+            ds = (held(kv, n, half, 0) * scales[group_of[n]]) * (held(kv, n, half, 1) - delta)
             ds_ref[kv, kept(n, half), tile] = ds.astype(jnp.bfloat16)
-        if n < REACH:
+
+    def send(kv):
+        kg = contract(ds_ref[kv], q_ref[kv], 1, 0) * SCALING
+        vg = contract(p_ref[kv, : REACH * rows], g_ref[kv], 1, 0)
+        for n in range(REACH):
             block = slice(n * rows, (n + 1) * rows)
-            kg = contract(ds_ref[kv, block], q_ref[kv], 1, 0) * SCALING
-            vg = contract(p_ref[kv, block], g_ref[kv], 1, 0)
-            term_refs[n][:, key_cols(kv)] = kg.astype(jnp.bfloat16)
-            term_refs[n][:, value_cols(kv, kv_heads)] = vg.astype(jnp.bfloat16)
+            term_refs[n][:, key_cols(kv)] = kg[block].astype(jnp.bfloat16)
+            term_refs[n][:, value_cols(kv, kv_heads)] = vg[block].astype(jnp.bfloat16)
 
     empty = jnp.zeros((part, cols), jnp.bfloat16)
     for kv in range(kv_heads):
-        for ref in (p_ref, ds_ref):
-            ref[kv, :part, cols:] = empty
-            ref[kv, (blocks * rows - part) :, :cols] = empty
-    scales = [[scores(kv, half) for half in range(HALVES)] for kv in range(kv_heads)]
-    deltas = [[attend(kv, half, scales[kv][half]) for half in range(HALVES)] for kv in range(kv_heads)]
-    for kv in range(kv_heads):
-        for n in range(blocks):
-            send(kv, n, scales[kv], deltas[kv])
-
-
-def own_kernel(q_ref, g_ref, att_ref, p_ref, ds_ref, *refs):
-    kv_refs, (att_out, qg_out, total_ref) = refs[:-3], refs[-3:]
+        ds_ref[kv, :part, cols:] = empty
+        p_ref[kv, :part, cols:] = empty
+        p_ref[kv, (blocks * rows - part) :, :cols] = empty
+        scales = [scores(kv, half) for half in range(HALVES)]
+        deltas = [attend(kv, half, scales[half]) for half in range(HALVES)]
+        for half in range(HALVES):
+            score_grads(kv, half, scales[half], deltas[half])
+        send(kv)
+
+
+def own_kernel(q_ref, g_ref, att_ref, p_ref, ds_ref, row_ref, p_near_ref, d_near_ref, *refs):
+    kv_refs, (att_out, qg_out, total_ref, own_scr) = refs[:-4], refs[-4:]
     rows = kv_refs[0].shape[0]
     kv_heads, all_cols = q_ref.shape[:2]
     group = all_cols // rows
     cols = all_cols // HALVES
     part = rows // HALVES
     remote = REACH * rows
+    own_scr[own_rows(rows, 0) :, :cols] = jnp.zeros((rows - part, cols), jnp.bfloat16)
     for kv in range(kv_heads):
         k = jnp.concatenate([r[:, key_cols(kv)] for r in kv_refs], axis=0)
-        total_ref[:, key_cols(kv)] = contract(ds_ref[kv, remote:], q_ref[kv], 1, 0) * SCALING
-        total_ref[:, value_cols(kv, kv_heads)] = contract(p_ref[kv, remote:], g_ref[kv], 1, 0)
         for half in range(HALVES):
             tile = slice(half * cols, (half + 1) * cols)
             start = half * part
-            stop = remote + own_rows(rows, half)
-            qg = contract(k[start:stop], ds_ref[kv, start:stop, tile], 0, 0) * SCALING
+            own = own_rows(rows, half)
+            near = slice(p_near_ref.shape[1] - rows, p_near_ref.shape[1] - rows + own)
+            p = p_near_ref[kv, near, tile] * row_ref[kv, 0:1, tile]
+            ds = p * (d_near_ref[kv, near, tile] - row_ref[kv, 1:2, tile])
+            own_scr[:own, tile] = ds.astype(jnp.bfloat16)
+            ds = jnp.concatenate([ds_ref[kv, start:, tile], own_scr[:own, tile]], axis=0)
+            qg = contract(k[start : remote + own], ds, 0, 0) * SCALING
             qg = qg.astype(jnp.bfloat16).T
             att = att_ref[kv, :, tile].T
             for n in range(group):
@@ -270,6 +289,8 @@
                 out = (slice(start, start + part), slice(h * HD, (h + 1) * HD))
                 att_out[out] = att[n * part : (n + 1) * part]
                 qg_out[out] = qg[n * part : (n + 1) * part]
+        total_ref[:, key_cols(kv)] = contract(own_scr[...], q_ref[kv], 1, 0) * SCALING
+        total_ref[:, value_cols(kv, kv_heads)] = contract(p_ref[kv, remote:], g_ref[kv], 1, 0)
 
 
 def add_kernel(total_ref, *refs):
@@ -287,7 +308,6 @@
     kv_width = 2 * key_states.shape[1]
     kv_heads = kv_width // (2 * HD)
     cols = rows * (width // HD // kv_heads)
-    near_keys = (REACH + 1 - FAR) * rows
     keys = (REACH + 1) * rows
     bf16, f32 = jnp.bfloat16, jnp.float32
     array = jax.ShapeDtypeStruct
@@ -296,7 +316,6 @@
     tall = array((kv_heads, cols, HD), bf16)
     turned = array((kv_heads, HD, cols), bf16)
     scores = array((kv_heads, keys, cols), bf16)
-    near_scores = array((kv_heads, near_keys, cols), f32)
     dma = pltpu.SemaphoreType.DMA
     work = 2 * HD * rows * cols * kv_heads
     first = (lax.axis_index(("ctx", "rep")) * rows).astype(jnp.int32).reshape(1)
@@ -327,20 +346,25 @@
         ],
     )
     blocks = [received[distance] if distance else own for distance in ORDER]
-    p, d, stat = call(
-        near_kernel,
-        "near",
-        [near_scores, near_scores, array((kv_heads, 2, cols), f32)],
-        [VMEM] * (4 + REACH - FAR),
-        [low, qt, gt] + blocks[FAR:],
-        2 * (REACH + 1 - FAR) * work,
-    )
-    *terms, att, p, ds = call(
+    partial = lambda name, before, part, distances: call(
+        functools.partial(partial_kernel, distances=distances),
+        name,
+        [array((kv_heads, len(part) * rows, cols), f32)] * 2
+        + [array((kv_heads, 2 + len(before), cols), f32)],
+        [VMEM] * (3 + len(before) + len(part)),
+        [low, qt, gt] + before + part,
+        2 * len(part) * work,
+    )
+    near = partial("near", [], blocks[FAR + MID :], ORDER[FAR + MID :])
+    mid = partial("mid", [near[2]], blocks[FAR : FAR + MID], ORDER[FAR : FAR + MID])
+    *terms, att, p, ds, rest = call(
         terms_kernel,
         "terms",
-        [narrow] * REACH + [turned, scores, scores],
-        [VMEM] * (9 + REACH),
-        [low, q, g, qt, gt, p, d, stat] + blocks,
+        [narrow] * REACH
+        + [turned, scores, array((kv_heads, REACH * rows, cols), bf16)]
+        + [array((kv_heads, 2, cols), f32)],
+        [VMEM] * (11 + REACH),
+        [low, q, g, qt, gt, *mid, *near[:2]] + blocks,
         (2 * FAR + 3 * REACH + 1) * work,
         [pltpu.VMEM((kv_heads, FAR * rows, cols), f32)] * 2,
     )
@@ -349,9 +373,10 @@
         own_kernel,
         "own",
         [wide, wide, array((rows, kv_width), f32)],
-        [VMEM] * (6 + REACH),
-        [q, g, att, p, ds] + blocks,
+        [VMEM] * (9 + REACH),
+        [q, g, att, p, ds, rest, near[0], near[1]] + blocks,
         (REACH + 3) * work,
+        [pltpu.VMEM((rows, cols), bf16)],
     )
     key_grad, value_grad = call(
         add_kernel,

time: 45.7 us -> 45.2 us (0.989)
  starting transfers between devices: 28.6 us -> 29.2 us
  waiting for transfers between devices: 5.28 us -> 4.71 us
    ppermute x8, waiting for transfers between devices: 5.28 us -> 4.71 us  [shifted(): return lax.ppermute(block, axes, route)]
    ppermute x8, starting transfers between devices: 28.6 us -> 29.2 us  [shifted(): return lax.ppermute(block, axes, route)]
    pallas_call x6 -> x7, Pallas kernels: 10.4 us -> 10.2 us  [call(): pl.pallas_call(kernel, out_shape=tuple(outs), in_specs=specs, out_specs=(...]
  transfers between devices with their start and end apart: 8 -> 8, of which waited for: 4 -> 4; matrix products, arithmetic and copies ran while one was open for 0% -> 0% of each run, Pallas kernels for 9% -> 11%
where the time goes in v4:
time: 45.2 us; the launch traced here: 44.9 us
  starting transfers between devices  29.2 us (65%)
  Pallas kernels  10.2 us (23%)
  waiting for transfers between devices  4.71 us (10%)
  between operations  0.75 us (2%)
    ppermute x8, starting transfers between devices, shifted(): return lax.ppermute(block, axes, route)  29.2 us
    pallas_call x7, Pallas kernels, call(): pl.pallas_call(kernel, out_shape=tuple(outs), in_specs=specs, out_specs=(...  10.2 us
    ppermute x8, waiting for transfers between devices, shifted(): return lax.ppermute(block, axes, route)  4.71 us
  transfers between devices with their start and end apart: 8, of which 4 were waited for; matrix products, arithmetic and copies ran while one was open for 0% of the time, Pallas kernels for 11%

profile of v4, /device:TPU:1, one launch (start us, length us, event | category | flops | bytes accessed | tf_op | source)
XLA Modules:
  0.0 44.9 jit_solution(13991432495273152021)
XLA Ops:
  0.6 1.0 %join.1.refs_1_.refs_9_.refs_4_ = bf16[192,512]{1,0:T(8,128)(2,1)S(1)} custom-call(bf16[192,256]{1,0:T(8,128)(2,1)} %k_hbm.1, bf16[192,256]{1,0:T(8,128)(2,1)} %v_hbm.1), custom_call_target="tpu_custom_call" | custom-call | bytes 393216 | tf_op jit(solution)/shard_map/join/pallas_call | solution.py:38
  1.6 5.5 %collective-permute-start = (bf16[192,512]{1,0:T(8,128)(2,1)S(1)}, bf16[192,512]{1,0:T(8,128)(2,1)S(1)}, u32[]{:S(2)}, u32[]{:S(2)}) collective-permute-start(bf16[192,512]{1,0:T(8,128)(2,1)S(1)} %join.1.refs_1_.refs_9_.refs_4_), channel_id=1, source_target_pairs={{0,2},{1,3},{2,16},{3,17},{16,18},{17,19},{18,32},{19,33},{32,34},... | collective-permute-start | bytes 589832 | tf_op jit(solution)/shard_map/ppermute | solution.py:27
  7.1 2.2 %collective-permute-start.1 = (bf16[192,512]{1,0:T(8,128)(2,1)S(1)}, bf16[192,512]{1,0:T(8,128)(2,1)S(1)}, u32[]{:S(2)}, u32[]{:S(2)}) collective-permute-start(bf16[192,512]{1,0:T(8,128)(2,1)S(1)} %join.1.refs_1_.refs_9_.refs_4_), channel_id=1, source_target_pairs={{0,1},{1,2},{2,3},{3,16},{16,17},{17,18},{18,19},{19,32},{32,33},{... | collective-permute-start | bytes 589832 | tf_op jit(solution)/shard_map/ppermute | solution.py:27
  9.3 6.1 %collective-permute-start.3 = (bf16[192,512]{1,0:T(8,128)(2,1)S(1)}, bf16[192,512]{1,0:T(8,128)(2,1)S(1)}, u32[]{:S(2)}, u32[]{:S(2)}) collective-permute-start(bf16[192,512]{1,0:T(8,128)(2,1)S(1)} %join.1.refs_1_.refs_9_.refs_4_), channel_id=1, source_target_pairs={{0,3},{1,16},{2,17},{3,18},{16,19},{17,32},{18,33},{19,34},{32,35}... | collective-permute-start | bytes 589832 | tf_op jit(solution)/shard_map/ppermute | solution.py:27
  15.4 1.9 %collective-permute-start.2 = (bf16[192,512]{1,0:T(8,128)(2,1)S(1)}, bf16[192,512]{1,0:T(8,128)(2,1)S(1)}, u32[]{:S(2)}, u32[]{:S(2)}) collective-permute-start(bf16[192,512]{1,0:T(8,128)(2,1)S(1)} %join.1.refs_1_.refs_9_.refs_4_), channel_id=1, source_target_pairs={{0,16},{1,17},{2,18},{3,19},{16,32},{17,33},{18,34},{19,35},{32,48... | collective-permute-start | bytes 589832 | tf_op jit(solution)/shard_map/ppermute | solution.py:27
  17.4 1.4 %load.1 = (bf16[2,768,128]{2,1,0:T(8,128)(2,1)S(1)}, bf16[2,768,128]{2,1,0:T(8,128)(2,1)S(1)}, bf16[2,128,768]{2,1,0:T(8,128)(2,1)S(1)}, bf16[2,128,768]{2,1,0:T(8,128)(2,1)S(1)}, s32[2,384]{1,0:T(2,128)S(1)}) custom-call(s32[1]{0:T(128)} %bitcast.first_ref, s32[1,255]{1,0:T(1,128)} %bitcast.2, bf16[192,1024]{1,0:T(8,128)(2,1)} %q_hbm.1, bf16[192,1024]{1,0:T(8,128)(2,1)} %g_hbm.1), custom_call_target="tpu_custom_call" | custom-call | bytes 2363392 | tf_op jit(solution)/shard_map/load/pallas_call | solution.py:38
  18.8 0.0 collective-permute-done.refs_0_.refs_8_.refs_3_
  18.8 0.9 %near.1 = (f32[2,384,768]{2,1,0:T(8,128)S(1)}, f32[2,384,768]{2,1,0:T(8,128)S(1)}, f32[2,2,768]{2,1,0:T(2,128)S(1)}) custom-call(s32[2,384]{1,0:T(2,128)S(1)} %get-tuple-element.30.low_ref, bf16[2,128,768]{2,1,0:T(8,128)(2,1)S(1)} %get-tuple-element.31.qt_ref, bf16[2,128,768]{2,1,0:T(8,128)(2,1)S(1)} %get-tuple-element.32.gt_ref, ...), custom_call_target="tpu_custom_call" | custom-call | flops 301989888 | bytes 5913600 | tf_op jit(solution)/shard_map/near/pallas_call | solution.py:38
  19.7 0.0 collective-permute-done.1.refs_1_.refs_7_.refs_2_
  19.7 0.5 %mid.1 = (f32[2,192,768]{2,1,0:T(8,128)S(1)}, f32[2,192,768]{2,1,0:T(8,128)S(1)}, f32[2,3,768]{2,1,0:T(4,128)S(1)}) custom-call(s32[2,384]{1,0:T(2,128)S(1)} %get-tuple-element.30.low_ref, bf16[2,128,768]{2,1,0:T(8,128)(2,1)S(1)} %get-tuple-element.31.qt_ref, bf16[2,128,768]{2,1,0:T(8,128)(2,1)S(1)} %get-tuple-element.32.gt_ref, ...), custom_call_target="tpu_custom_call" | custom-call | flops 150994944 | bytes 3376128 | tf_op jit(solution)/shard_map/mid/pallas_call | solution.py:38
  20.3 0.0 collective-permute-done.3.refs_6_.refs_1_
  20.3 1.6 %collective-permute-done.2.refs_5_.refs_0_ = bf16[192,512]{1,0:T(8,128)(2,1)S(1)} collective-permute-done((bf16[192,512]{1,0:T(8,128)(2,1)S(1)}, bf16[192,512]{1,0:T(8,128)(2,1)S(1)}, u32[]{:S(2)}, u32[]{:S(2)}) %collective-permute-start.2) | collective-permute-done | bytes 196640 | tf_op jit(solution)/shard_map/ppermute | solution.py:27
  21.9 3.7 %terms.1 = (bf16[192,512]{1,0:T(8,128)(2,1)S(1)}, bf16[192,512]{1,0:T(8,128)(2,1)S(1)}, bf16[192,512]{1,0:T(8,128)(2,1)S(1)}, bf16[192,512]{1,0:T(8,128)(2,1)S(1...) custom-call(s32[2,384]{1,0:T(2,128)S(1)} %get-tuple-element.30.low_r, ...), custom_call_target="tpu_custom_call" | custom-call | flops 1283457024 | bytes 16155648 | tf_op jit(solution)/shard_map/terms/pallas_call | solution.py:38
  25.6 5.3 %collective-permute-start.4 = (bf16[192,512]{1,0:T(8,128)(2,1)S(1)}, bf16[192,512]{1,0:T(8,128)(2,1)S(1)}, u32[]{:S(2)}, u32[]{:S(2)}) collective-permute-start(bf16[192,512]{1,0:T(8,128)(2,1)S(1)} %get-tuple-element.46), channel_id=1, source_target_pairs={{2,0},{3,1},{16,2},{17,3},{18,16},{19,17},{32,18},{33,19},{34,32},... | collective-permute-start | bytes 589832 | tf_op jit(solution)/shard_map/ppermute | solution.py:27
  30.9 4.3 %collective-permute-start.5 = (bf16[192,512]{1,0:T(8,128)(2,1)S(1)}, bf16[192,512]{1,0:T(8,128)(2,1)S(1)}, u32[]{:S(2)}, u32[]{:S(2)}) collective-permute-start(bf16[192,512]{1,0:T(8,128)(2,1)S(1)} %get-tuple-element.47), channel_id=1, source_target_pairs={{1,0},{2,1},{3,2},{16,3},{17,16},{18,17},{19,18},{32,19},{33,32},{... | collective-permute-start | bytes 589832 | tf_op jit(solution)/shard_map/ppermute | solution.py:27
  35.2 1.9 %collective-permute-start.6 = (bf16[192,512]{1,0:T(8,128)(2,1)S(1)}, bf16[192,512]{1,0:T(8,128)(2,1)S(1)}, u32[]{:S(2)}, u32[]{:S(2)}) collective-permute-start(bf16[192,512]{1,0:T(8,128)(2,1)S(1)} %get-tuple-element.48), channel_id=1, source_target_pairs={{3,0},{16,1},{17,2},{18,3},{19,16},{32,17},{33,18},{34,19},{35,32}... | collective-permute-start | bytes 589832 | tf_op jit(solution)/shard_map/ppermute | solution.py:27
  37.1 1.9 %collective-permute-start.7 = (bf16[192,512]{1,0:T(8,128)(2,1)S(1)}, bf16[192,512]{1,0:T(8,128)(2,1)S(1)}, u32[]{:S(2)}, u32[]{:S(2)}) collective-permute-start(bf16[192,512]{1,0:T(8,128)(2,1)S(1)} %get-tuple-element.49), channel_id=1, source_target_pairs={{16,0},{17,1},{18,2},{19,3},{32,16},{33,17},{34,18},{35,19},{48,32... | collective-permute-start | bytes 589832 | tf_op jit(solution)/shard_map/ppermute | solution.py:27
  39.0 2.0 %own.1 = (bf16[192,1024]{1,0:T(8,128)(2,1)}, bf16[192,1024]{1,0:T(8,128)(2,1)}, f32[192,512]{1,0:T(8,128)S(1)}) custom-call(bf16[2,768,128]{2,1,0:T(8,128)(2,1)S(1)} %get-tuple-element.28.q_ref, bf16[2,768,128]{2,1,0:T(8,128)(2,1)S(1)} %get-tuple-element.29.g_ref, bf16[2,128,768]{2,1,0:T(8,128)(2,1)S(1)} %get-tuple-element.39.att_ref, ...), custom_call_target="tpu_custom_call" | custom-call | flops 528482304 | bytes 13381632 | tf_op jit(solution)/shard_map/own/pallas_call | solution.py:38
  41.0 0.0 collective-permute-done.4.refs_0_
  41.0 0.7 %collective-permute-done.5.refs_1_ = bf16[192,512]{1,0:T(8,128)(2,1)S(1)} collective-permute-done((bf16[192,512]{1,0:T(8,128)(2,1)S(1)}, bf16[192,512]{1,0:T(8,128)(2,1)S(1)}, u32[]{:S(2)}, u32[]{:S(2)}) %collective-permute-start.5) | collective-permute-done | bytes 196640 | tf_op jit(solution)/shard_map/ppermute | solution.py:27
  41.7 1.1 %collective-permute-done.6.refs_2_ = bf16[192,512]{1,0:T(8,128)(2,1)S(1)} collective-permute-done((bf16[192,512]{1,0:T(8,128)(2,1)S(1)}, bf16[192,512]{1,0:T(8,128)(2,1)S(1)}, u32[]{:S(2)}, u32[]{:S(2)}) %collective-permute-start.6) | collective-permute-done | bytes 196640 | tf_op jit(solution)/shard_map/ppermute | solution.py:27
  42.8 1.3 %collective-permute-done.7.refs_3_ = bf16[192,512]{1,0:T(8,128)(2,1)S(1)} collective-permute-done((bf16[192,512]{1,0:T(8,128)(2,1)S(1)}, bf16[192,512]{1,0:T(8,128)(2,1)S(1)}, u32[]{:S(2)}, u32[]{:S(2)}) %collective-permute-start.7) | collective-permute-done | bytes 196640 | tf_op jit(solution)/shard_map/ppermute | solution.py:27
  44.1 0.8 %add.5 = (bf16[192,256]{1,0:T(8,128)(2,1)}, bf16[192,256]{1,0:T(8,128)(2,1)}) custom-call(f32[192,512]{1,0:T(8,128)S(1)} %get-tuple-element.45.total_ref, bf16[192,512]{1,0:T(8,128)(2,1)S(1)} %collective-permute-done.4.refs_0_, bf16[192,512]{1,0:T(8,128)(2,1)S(1)} %collective-permute-done.5.refs_1_, bf16[192,512]{1,0:T(8,128)(2,1)S(1)} %collective-permute-done.6.refs_2_, ...), custom_call_target="tpu_custom_call" | custom-call | bytes 1376256 | tf_op jit(solution)/shard_map/add/pallas_call | solution.py:38
Async XLA Ops:
  1.6 17.2 %collective-permute-start = (bf16[192,512]{1,0:T(8,128)(2,1)S(1)}, bf16[192,512]{1,0:T(8,128)(2,1)S(1)}, u32[]{:S(2)}, u32[]{:S(2)}) collective-permute-start(bf16[192,512]{1,0:T(8,128)(2,1)S(1)} %join.1.refs_1_.refs_9_.refs_4_), channel_id=1, source_target_pairs={{0,2},{1,3},{2,16},{3,17},{16,18},{17,19},{18,32},{19,33},{32,34},... | collective-permute-start | bytes 589832 | tf_op jit(solution)/shard_map/ppermute | solution.py:27
  7.1 12.6 %collective-permute-start.1 = (bf16[192,512]{1,0:T(8,128)(2,1)S(1)}, bf16[192,512]{1,0:T(8,128)(2,1)S(1)}, u32[]{:S(2)}, u32[]{:S(2)}) collective-permute-start(bf16[192,512]{1,0:T(8,128)(2,1)S(1)} %join.1.refs_1_.refs_9_.refs_4_), channel_id=1, source_target_pairs={{0,1},{1,2},{2,3},{3,16},{16,17},{17,18},{18,19},{19,32},{32,33},{... | collective-permute-start | bytes 589832 | tf_op jit(solution)/shard_map/ppermute | solution.py:27
  9.3 11.0 %collective-permute-start.3 = (bf16[192,512]{1,0:T(8,128)(2,1)S(1)}, bf16[192,512]{1,0:T(8,128)(2,1)S(1)}, u32[]{:S(2)}, u32[]{:S(2)}) collective-permute-start(bf16[192,512]{1,0:T(8,128)(2,1)S(1)} %join.1.refs_1_.refs_9_.refs_4_), channel_id=1, source_target_pairs={{0,3},{1,16},{2,17},{3,18},{16,19},{17,32},{18,33},{19,34},{32,35}... | collective-permute-start | bytes 589832 | tf_op jit(solution)/shard_map/ppermute | solution.py:27
  15.4 6.4 %collective-permute-start.2 = (bf16[192,512]{1,0:T(8,128)(2,1)S(1)}, bf16[192,512]{1,0:T(8,128)(2,1)S(1)}, u32[]{:S(2)}, u32[]{:S(2)}) collective-permute-start(bf16[192,512]{1,0:T(8,128)(2,1)S(1)} %join.1.refs_1_.refs_9_.refs_4_), channel_id=1, source_target_pairs={{0,16},{1,17},{2,18},{3,19},{16,32},{17,33},{18,34},{19,35},{32,48... | collective-permute-start | bytes 589832 | tf_op jit(solution)/shard_map/ppermute | solution.py:27
  25.6 15.4 %collective-permute-start.4 = (bf16[192,512]{1,0:T(8,128)(2,1)S(1)}, bf16[192,512]{1,0:T(8,128)(2,1)S(1)}, u32[]{:S(2)}, u32[]{:S(2)}) collective-permute-start(bf16[192,512]{1,0:T(8,128)(2,1)S(1)} %get-tuple-element.46), channel_id=1, source_target_pairs={{2,0},{3,1},{16,2},{17,3},{18,16},{19,17},{32,18},{33,19},{34,32},... | collective-permute-start | bytes 589832 | tf_op jit(solution)/shard_map/ppermute | solution.py:27
  30.9 10.8 %collective-permute-start.5 = (bf16[192,512]{1,0:T(8,128)(2,1)S(1)}, bf16[192,512]{1,0:T(8,128)(2,1)S(1)}, u32[]{:S(2)}, u32[]{:S(2)}) collective-permute-start(bf16[192,512]{1,0:T(8,128)(2,1)S(1)} %get-tuple-element.47), channel_id=1, source_target_pairs={{1,0},{2,1},{3,2},{16,3},{17,16},{18,17},{19,18},{32,19},{33,32},{... | collective-permute-start | bytes 589832 | tf_op jit(solution)/shard_map/ppermute | solution.py:27
  35.2 7.6 %collective-permute-start.6 = (bf16[192,512]{1,0:T(8,128)(2,1)S(1)}, bf16[192,512]{1,0:T(8,128)(2,1)S(1)}, u32[]{:S(2)}, u32[]{:S(2)}) collective-permute-start(bf16[192,512]{1,0:T(8,128)(2,1)S(1)} %get-tuple-element.48), channel_id=1, source_target_pairs={{3,0},{16,1},{17,2},{18,3},{19,16},{32,17},{33,18},{34,19},{35,32}... | collective-permute-start | bytes 589832 | tf_op jit(solution)/shard_map/ppermute | solution.py:27
  37.1 7.0 %collective-permute-start.7 = (bf16[192,512]{1,0:T(8,128)(2,1)S(1)}, bf16[192,512]{1,0:T(8,128)(2,1)S(1)}, u32[]{:S(2)}, u32[]{:S(2)}) collective-permute-start(bf16[192,512]{1,0:T(8,128)(2,1)S(1)} %get-tuple-element.49), channel_id=1, source_target_pairs={{16,0},{17,1},{18,2},{19,3},{32,16},{33,17},{34,18},{35,19},{48,32... | collective-permute-start | bytes 589832 | tf_op jit(solution)/shard_map/ppermute | solution.py:27
